TPU v7x, 32 devices: a whole 2x2x4 slice. The times are simulated.
32 devices in a mesh: row: 4 (over y, x), col: 4 (over z), layer: 2 (over core).
Axes of the slice: x: 2, y: 2, z: 4, core: 2. Of those that a mesh axis runs over, the one named last changes fastest.
Arguments:
- earlier_warming_amount: float32 [8, 512, 512], P('layer', 'row', 'col'), may hold values from -2 to 2
- conductive_capability: float32 [8, 512, 512], P('layer', 'row', 'col'), may hold values from 0.5 to 2
- thermal_mass_timewise: float32 [8, 512, 512], P('layer', 'row', 'col'), may hold values from 0.5 to 2
- toggling_wattage_map: bfloat16 [32, 64, 4096], P(('row', 'col', 'layer')), may hold values from 0.049804688 to 1
- baseline_loss_wattage: bfloat16 [32, 64, 4096], P(('row', 'col', 'layer')), may hold values from 0.049804688 to 1
- receiving_panel: int32 [32, 64, 1], P(('row', 'col', 'layer')), may hold values from 0 to 15; in each aligned block of 64 rows (0 to 63, 64 to 127, ..., all dimensions but the last counted through in order) at most 4 rows name the same one
- subsquare_placement: int32 [32, 64], P(('row', 'col', 'layer')), may hold values from 0 to 3
- holder_chip_module: int32 [32, 64], P(('row', 'col', 'layer')), may hold values from 0 to 15, never falling along the last dimension, each value on 1 to 8 neighbouring positions
- module_tier_order: int32 [32, 16], P(('row', 'col', 'layer')), may hold values from 0 to 3
- warming_sensitivity: float32 [32, 16], P(('row', 'col', 'layer')), may hold values from 0.5 to 2
Outputs:
- new_temperature: float32 [8, 512, 512], P('layer', 'row', 'col')
- supplied_wattage_density: float32 [8, 512, 512], P('layer', 'row', 'col')
Inputs may be any that keep to these rules, and one draw needn't show every extreme that they name: `receiving_panel`: the tile is numbered row tile times the number of column tiles plus column tile, inside the owning device's layer group; among the slots of one device at most 4 name the same tile, and exactly 4 do on some device in every draw. `subsquare_placement`: row-major over the tile's patch rows and patch columns. `holder_chip_module`: never falls along a device's slots; every block of a device has 1 to 8 slots.
All inputs are finite; a program needn't handle non-finite values.
Results may differ from a plain program's by a relative error of at most 0.0012.
Values may be sent and summed in bfloat16 or wider, within the bound.
A program may use at most 64 MiB of HBM per device.

v0:
```python
import jax
import jax.numpy as jnp
from jax import lax
from jax.sharding import PartitionSpec as P

SUBSQUARE_EXTENT = 64
SWEEPS = 3
CAP = 4


eig_low = 0.1
eig_high = 2.0


def padded_2(cells, sides, width):
    for axis, dim in sides:
        count = lax.axis_size(axis)
        ends = count - 1
        head = lax.slice_in_dim(cells, 0, width, axis=dim)
        tail = lax.slice_in_dim(cells, cells.shape[dim] - width, cells.shape[dim], axis=dim)
        cells = jnp.concatenate(
            [
                lax.ppermute(tail, axis, [(i, (i + 1) % count) for i in range(ends)]),
                cells,
                lax.ppermute(head, axis, [((i + 1) % count, i) for i in range(ends)]),
            ],
            axis=dim,
        )
    return cells


def neighbours(padded):
    return [
        padded[2:, 1:-1, 1:-1],
        padded[:-2, 1:-1, 1:-1],
        padded[1:-1, 2:, 1:-1],
        padded[1:-1, :-2, 1:-1],
        padded[1:-1, 1:-1, 2:],
        padded[1:-1, 1:-1, :-2],
    ]


def face_terms(padded_cond):
    center = padded_cond[1:-1, 1:-1, 1:-1]
    return [0.5 * (center + beside) for beside in neighbours(padded_cond)]


def diagonal_of(thermal_mass_timewise, nearby_conductance_factors):
    running = thermal_mass_timewise
    for face_term in nearby_conductance_factors:
        running = running + face_term
    return running


def linear_mapping_result(padded, nearby_conductance_factors, linear_pivot_coefficients):
    result = linear_pivot_coefficients * padded[1:-1, 1:-1, 1:-1]
    for face_term, beside in zip(nearby_conductance_factors, neighbours(padded)):
        result = result - face_term * beside
    return result


def trim(array, margin):
    if margin == 0:
        return array
    return array[margin:-margin, margin:-margin, margin:-margin]


def exact_dot(former, latter):
    return jnp.dot(
        former, latter, precision=lax.Precision.HIGHEST, preferred_element_type=jnp.float32
    )


def shards(
    earlier_warming_amount,
    conductive_capability,
    thermal_mass_timewise,
    toggling_wattage_map,
    baseline_loss_wattage,
    receiving_panel,
    subsquare_placement,
    holder_chip_module,
    module_tier_order,
    warming_sensitivity,
):
    tile_total = lax.axis_size(("row", "col"))
    number_sheetwise, number_lengthwise, tier_total_number = earlier_warming_amount.shape
    in_plane = number_lengthwise // SUBSQUARE_EXTENT * (tier_total_number // SUBSQUARE_EXTENT)
    tile_patches = number_sheetwise * in_plane
    target = receiving_panel[0, :, 0]
    tile_hits = (target[:, None] == jnp.arange(tile_total, dtype=jnp.int32)[None, :]).astype(
        jnp.int32
    )
    order_rank = jnp.sum(jnp.cumsum(tile_hits, axis=0) * tile_hits, axis=1) - 1
    slot_place = target * CAP + order_rank
    placing = (
        jnp.arange(tile_total * CAP, dtype=jnp.int32)[:, None] == slot_place[None, :]
    ).astype(jnp.float32)
    placing_half = placing.astype(jnp.bfloat16)
    local_block = holder_chip_module[0]
    block_total = module_tier_order.shape[1]
    block_match = local_block[:, None] == jnp.arange(block_total, dtype=jnp.int32)[None, :]
    member = jnp.transpose(block_match.astype(jnp.float32))
    slot_layer = jnp.sum(jnp.where(block_match, module_tier_order[0][None, :], 0), axis=1)
    position = slot_layer * in_plane + subsquare_placement[0]
    position_buf = exact_dot(placing, (position + 1).astype(jnp.float32)) - 1.0
    tile_means = (
        earlier_warming_amount.reshape(
            number_sheetwise,
            number_lengthwise // SUBSQUARE_EXTENT,
            SUBSQUARE_EXTENT,
            tier_total_number // SUBSQUARE_EXTENT,
            SUBSQUARE_EXTENT,
        )
        .mean(axis=(2, 4))
        .reshape(tile_patches)
    )
    block_sizes = jnp.sum(member, axis=1)
    patch_ids = jnp.arange(tile_patches, dtype=jnp.int32).astype(jnp.float32)
    dyn_send = (
        jnp.dot(placing_half, toggling_wattage_map[0], preferred_element_type=jnp.float32)
        .astype(jnp.bfloat16)
        .reshape(tile_total, CAP, -1)
    )
    leak_send = (
        jnp.dot(placing_half, baseline_loss_wattage[0], preferred_element_type=jnp.float32)
        .astype(jnp.bfloat16)
        .reshape(tile_total, CAP, -1)
    )
    place_send = position_buf.astype(jnp.bfloat16).reshape(tile_total, CAP)
    dyn_recv, leak_recv, place_recv = (
        lax.all_to_all(dyn_send, ("row", "col"), split_axis=0, concat_axis=0, tiled=True),
        lax.all_to_all(leak_send, ("row", "col"), split_axis=0, concat_axis=0, tiled=True),
        lax.all_to_all(place_send, ("row", "col"), split_axis=0, concat_axis=0, tiled=True),
    )
    selector = (patch_ids[:, None] == place_recv.reshape(-1).astype(jnp.float32)[None, :]).astype(
        jnp.float32
    )
    means_there = exact_dot(tile_means, selector).reshape(tile_total, CAP)
    means_home = lax.all_to_all(
        means_there, ("row", "col"), split_axis=0, concat_axis=0, tiled=True
    )
    block_means = exact_dot(member, exact_dot(means_home.reshape(-1), placing)) / block_sizes
    slot_factor = exact_dot(jnp.exp(warming_sensitivity[0] * block_means), member)
    factor_send = exact_dot(placing, slot_factor).reshape(tile_total, CAP)
    factor_recv = lax.all_to_all(
        factor_send, ("row", "col"), split_axis=0, concat_axis=0, tiled=True
    )
    slot_power = (
        dyn_recv.reshape(tile_total * CAP, -1).astype(jnp.float32)
        + factor_recv.reshape(-1)[:, None]
        * leak_recv.reshape(tile_total * CAP, -1).astype(jnp.float32)
    ).astype(jnp.bfloat16)
    footprint_wattage = jnp.dot(
        selector.astype(jnp.bfloat16), slot_power, preferred_element_type=jnp.float32
    )
    supplied_wattage_density = (
        footprint_wattage.reshape(
            number_sheetwise,
            number_lengthwise // SUBSQUARE_EXTENT,
            tier_total_number // SUBSQUARE_EXTENT,
            SUBSQUARE_EXTENT,
            SUBSQUARE_EXTENT,
        )
        .transpose(0, 1, 3, 2, 4)
        .reshape(number_sheetwise, number_lengthwise, tier_total_number)
    )
    middle = (eig_low + eig_high) / 2.0
    spread = (eig_high - eig_low) / 2.0
    ratio_sigma = middle / spread
    weight_now = 1.0 / ratio_sigma
    width = SWEEPS
    whole = padded_2(
        jnp.stack(
            [
                earlier_warming_amount,
                conductive_capability,
                thermal_mass_timewise,
                supplied_wattage_density,
            ]
        ),
        (("row", 2), ("col", 3), ("layer", 1)),
        width,
    )
    padded_temp = whole[0]
    nearby_conductance_factors = face_terms(whole[1])
    inner_cap = trim(whole[2], 1)
    linear_pivot_coefficients = diagonal_of(inner_cap, nearby_conductance_factors)
    inside = inner_cap > 0.0
    safe_diag = jnp.where(inside, linear_pivot_coefficients, 1.0)
    right_side = inner_cap * trim(padded_temp, 1) + trim(whole[3], 1)
    remaining_imbalance = right_side - linear_mapping_result(
        padded_temp, nearby_conductance_factors, linear_pivot_coefficients
    )
    direction = jnp.where(inside, remaining_imbalance / (safe_diag * middle), 0.0)
    iterate_guess = trim(padded_temp, width)
    margin = width - 1
    for sweep in range(SWEEPS):
        iterate_guess = iterate_guess + trim(direction, margin)
        if sweep < SWEEPS - 1:
            nearby_conductance_factors = [
                trim(face_term, 1) for face_term in nearby_conductance_factors
            ]
            linear_pivot_coefficients = trim(linear_pivot_coefficients, 1)
            inside = trim(inside, 1)
            safe_diag = trim(safe_diag, 1)
            remaining_imbalance = trim(remaining_imbalance, 1) - linear_mapping_result(
                direction, nearby_conductance_factors, linear_pivot_coefficients
            )
            weight_new = 1.0 / (2.0 * ratio_sigma - weight_now)
            direction = jnp.where(
                inside,
                weight_new * weight_now * trim(direction, 1)
                + 2.0 * weight_new / spread * (remaining_imbalance / safe_diag),
                0.0,
            )
            weight_now = weight_new
            margin = margin - 1
    return (iterate_guess, supplied_wattage_density)


def solution(mesh):
    return jax.shard_map(
        shards,
        mesh=mesh,
        in_specs=(
            P("layer", "row", "col"),
            P("layer", "row", "col"),
            P("layer", "row", "col"),
            P(("row", "col", "layer"), None, None),
            P(("row", "col", "layer"), None, None),
            P(("row", "col", "layer"), None, None),
            P(("row", "col", "layer"), None),
            P(("row", "col", "layer"), None),
            P(("row", "col", "layer"), None),
            P(("row", "col", "layer"), None),
        ),
        out_specs=(P("layer", "row", "col"), P("layer", "row", "col")),
        check_vma=False,
    )
```

profile of v0, /device:TPU:0, one launch (start us, length us, event | category | flops | bytes accessed | tf_op | source)
XLA Modules:
  0.0 140.6 jit_solution(15268636562175830727)
XLA Ops:
  5.4 8.3 %all-to-all-start = ((bf16[16,1,4]{2,1,0:T(2,128)(2,1)}), bf16[16,1,4]{2,1,0:T(2,128)(2,1)S(1)}, u32[]{:S(2)}, u32[]{:S(2)}) async-start(bf16[16,1,4]{2,1,0:T(2,128)(2,1)} %all_to_all.32), calls=%async_computation | async-start | bytes 16384 | tf_op jit(solution)/shard_map/all_to_all | solution.py:134
  15.5 5.5 %all-to-all-done = bf16[16,1,4]{2,1,0:T(2,128)(2,1)S(1)} async-done(((bf16[16,1,4]{2,1,0:T(2,128)(2,1)}), bf16[16,1,4]{2,1,0:T(2,128)(2,1)S(1)}, u32[]{:S(2)}, u32[]{:S(2)}) %all-to-all-start) | async-done | bytes 160 | tf_op jit(solution)/shard_map/all_to_all | solution.py:134
  21.8 3.5 %all-to-all-start.2 = ((f32[16,1,4]{2,1,0:T(1,128)}), f32[16,1,4]{2,1,0:T(1,128)S(1)}, u32[]{:S(2)}, u32[]{:S(2)}) async-start(f32[16,1,4]{2,1,0:T(1,128)} %bitcast.35), calls=%async_computation.2 | async-start | bytes 16384 | tf_op jit(solution)/shard_map/all_to_all | solution.py:140
  25.4 7.1 %all-to-all-done.2 = f32[16,1,4]{2,1,0:T(1,128)S(1)} async-done(((f32[16,1,4]{2,1,0:T(1,128)}), f32[16,1,4]{2,1,0:T(1,128)S(1)}, u32[]{:S(2)}, u32[]{:S(2)}) %all-to-all-start.2) | async-done | bytes 288 | tf_op jit(solution)/shard_map/all_to_all | solution.py:140
  35.0 3.5 %all-to-all-start.3 = ((f32[16,1,4]{2,1,0:T(1,128)}), f32[16,1,4]{2,1,0:T(1,128)S(1)}, u32[]{:S(2)}, u32[]{:S(2)}) async-start(f32[16,1,4]{2,1,0:T(1,128)} %bitcast.23), calls=%async_computation.3 | async-start | bytes 16384 | tf_op jit(solution)/shard_map/all_to_all | solution.py:146
  39.8 5.9 %all-to-all-done.3 = f32[16,1,4]{2,1,0:T(1,128)S(1)} async-done(((f32[16,1,4]{2,1,0:T(1,128)}), f32[16,1,4]{2,1,0:T(1,128)S(1)}, u32[]{:S(2)}, u32[]{:S(2)}) %all-to-all-start.3) | async-done | bytes 288 | tf_op jit(solution)/shard_map/all_to_all | solution.py:146
  45.6 3.6 %all-to-all-start.1 = ((bf16[16,4,4096]{2,1,0:T(4,128)(2,1)}), bf16[16,4,4096]{2,1,0:T(4,128)(2,1)S(1)}, u32[]{:S(2)}, u32[]{:S(2)}) async-start(bf16[16,4,4096]{2,1,0:T(4,128)(2,1)} %reshape.105), calls=%async_computation.1 | async-start | bytes 1048576 | tf_op jit(solution)/shard_map/all_to_all | solution.py:132
  50.5 11.4 %all-to-all-done.1 = bf16[16,4,4096]{2,1,0:T(4,128)(2,1)S(1)} async-done(((bf16[16,4,4096]{2,1,0:T(4,128)(2,1)}), bf16[16,4,4096]{2,1,0:T(4,128)(2,1)S(1)}, u32[]{:S(2)}, u32[]{:S(2)}) %all-to-all-start.1) | async-done | bytes 524320 | tf_op jit(solution)/shard_map/all_to_all | solution.py:132
  61.9 3.6 %all-to-all-start.4 = ((bf16[16,4,4096]{2,1,0:T(4,128)(2,1)}), bf16[16,4,4096]{2,1,0:T(4,128)(2,1)S(1)}, u32[]{:S(2)}, u32[]{:S(2)}) async-start(bf16[16,4,4096]{2,1,0:T(4,128)(2,1)} %reshape.108), calls=%async_computation.4 | async-start | bytes 1048576 | tf_op jit(solution)/shard_map/all_to_all | solution.py:133
  66.5 12.8 %all-to-all-done.4 = bf16[16,4,4096]{2,1,0:T(4,128)(2,1)S(1)} async-done(((bf16[16,4,4096]{2,1,0:T(4,128)(2,1)}), bf16[16,4,4096]{2,1,0:T(4,128)(2,1)S(1)}, u32[]{:S(2)}, u32[]{:S(2)}) %all-to-all-start.4) | async-done | bytes 524320 | tf_op jit(solution)/shard_map/all_to_all | solution.py:133
  82.1 2.2 %collective-permute-start = (f32[4,4,3,128]{3,2,1,0:T(4,128)S(1)}, f32[4,4,3,128]{3,2,1,0:T(4,128)}, u32[]{:S(2)}, u32[]{:S(2)}) collective-permute-start(f32[4,4,3,128]{3,2,1,0:T(4,128)S(1)} %get-tuple-element.22), channel_id=1, source_target_pairs={{0,8},{8,16},{16,24},{1,9},{9,17},{17,25},{2,10},{10,18},{18,26},{... | collective-permute-start | bytes 73736 | tf_op jit(solution)/shard_map/ppermute | solution.py:23
  85.5 4.5 %collective-permute-done.1 = f32[4,4,3,128]{3,2,1,0:T(4,128)S(1)} collective-permute-done((f32[4,4,3,128]{3,2,1,0:T(4,128)S(1)}, f32[4,4,3,128]{3,2,1,0:T(4,128)S(1)}, u32[]{:S(2)}, u32[]{:S(2)}) %collective-permute-start.1) | collective-permute-done | bytes 24608 | tf_op jit(solution)/shard_map/ppermute | solution.py:25
  92.9 1.9 %copy.48 = f32[4,4,134,3]{2,1,3,0:T(4,128)S(1)} copy(f32[4,4,134,3]{3,2,1,0:T(8,128)} %get-tuple-element.20) | data formatting | bytes 51456 | tf_op jit(solution)/shard_map/slice | solution.py:20
  94.8 2.7 %collective-permute-start.2 = (f32[4,4,134,3]{2,1,3,0:T(4,128)S(1)}, f32[4,4,134,3]{2,1,3,0:T(4,128)S(1)}, u32[]{:S(2)}, u32[]{:S(2)}) collective-permute-start(f32[4,4,134,3]{2,1,3,0:T(4,128)S(1)} %copy.48), channel_id=1, source_target_pairs={{0,2},{2,4},{4,6},{1,3},{3,5},{5,7},{8,10},{10,12},{12,14},{9,11},... | collective-permute-start | bytes 77192 | tf_op jit(solution)/shard_map/ppermute | solution.py:23
  99.8 4.4 %collective-permute-done.3 = f32[4,4,134,3]{2,1,3,0:T(4,128)} collective-permute-done((f32[4,4,134,3]{2,1,3,0:T(4,128)S(1)}, f32[4,4,134,3]{2,1,3,0:T(4,128)}, u32[]{:S(2)}, u32[]{:S(2)}) %collective-permute-start.3) | collective-permute-done | bytes 25760 | tf_op jit(solution)/shard_map/ppermute | solution.py:25
  105.4 2.0 %pad_maximum_fusion.1 = f32[4,4,134,134]{3,2,1,0:T(8,128)S(1)} fusion(f32[4,4,134,3]{3,2,1,0:T(8,128)S(1)} %copy.51, f32[4,4,3,128]{3,2,1,0:T(4,128)} %copy-done.7, f32[1,4,128,128]{3,2,1,0:T(8,128)S(1)} %stack_reshape.3, f32[1,4,128,128]{3,2,1,0:T(8,128)S(1)} %bitcast.93, f32[1,4,128,128]{3,2,1,0:T(8,128)} %bitcast.95, f32[1,4,128,128]{3,2,1,0:T(8,128)S(1)} %bitcast.89, ...), kind=kLoop, calls=%fused_computation.3 | loop fusion | flops 2011072 | bytes 2298368 | tf_op jit(solution)/shard_map/concatenate | solution.py:21
  107.6 1.8 %copy.53 = f32[4,3,134,134]{3,0,2,1:T(4,128)} copy(f32[4,3,134,134]{3,2,1,0:T(8,128)S(1)} %get-tuple-element.19) | data formatting | bytes 1723776 | tf_op jit(solution)/shard_map/slice | solution.py:19
  110.8 1.8 %copy.52 = f32[4,3,134,134]{3,0,2,1:T(4,128)} copy(f32[4,3,134,134]{3,2,1,0:T(8,128)S(1)} %get-tuple-element.18) | data formatting | bytes 1723776 | tf_op jit(solution)/shard_map/slice | solution.py:20
  112.6 5.4 %collective-permute-start.4 = (f32[4,3,134,134]{3,0,2,1:T(4,128)}, f32[4,3,134,134]{3,0,2,1:T(4,128)}, u32[]{:S(2)}, u32[]{:S(2)}) collective-permute-start(f32[4,3,134,134]{3,0,2,1:T(4,128)} %copy.52), channel_id=1, source_target_pairs={{0,1},{2,3},{4,5},{6,7},{8,9},{10,11},{12,13},{14,15},{16,17},{18,... | collective-permute-start | bytes 2585672 | tf_op jit(solution)/shard_map/ppermute | solution.py:23
  118.0 2.0 %reshape.109 = f32[4,128,128]{2,1,0:T(8,128)} reshape(f32[4,2,64,2,64]{4,3,2,1,0:T(2,128)} %copy-done.2) | data formatting | bytes 524288 | tf_op jit(solution)/shard_map/reshape | solution.py:166
  123.6 6.1 %pad_maximum_fusion = f32[4,10,134,134]{3,2,1,0:T(8,128)S(1)} fusion(f32[4,3,134,134]{3,2,1,0:T(8,128)S(1)} %copy.55, f32[4,4,134,3]{3,2,1,0:T(8,128)S(1)} %copy.51, f32[4,4,3,128]{3,2,1,0:T(4,128)S(1)} %copy-done.8, f32[1,4,128,128]{3,2,1,0:T(8,128)S(1)} %stack_reshape.3, f32[1,4,128,128]{3,2,1,0:T(8,128)S(1)} %bitcast.94, f32[1,4,128,128]{3,2,1,0:T(8,128)S(1)} %bitcast.98, ...), kind=kLoop, calls=%fused_computation | loop fusion | flops 6464160 | bytes 5745920 | tf_op jit(solution)/shard_map/concatenate | solution.py:21
  130.1 4.6 %divide_select_fusion = (f32[8,132,132]{2,1,0:T(8,128)S(1)}, f32[8,132,132]{2,1,0:T(8,128)S(1)}, f32[8,132,132]{2,1,0:T(8,128)S(1)}, f32[8,132,132]{2,1,0:T(8,12...) fusion(f32[10,134,134]{2,1,0:T(8,128)S(1)} %get-tuple-element.1, ...), kind=kLoop, calls=%fused_computation.36 | loop fusion | flops 5436288 | bytes 14078592 | tf_op jit(solution)/shard_map/jit(_where)/select_n | solution.py:195
  134.9 3.6 %fusion.21 = (f32[6,130,130]{2,1,0:T(8,128)S(1)}, f32[6,130,130]{2,1,0:T(8,128)S(1)}) fusion(f32[8,132,132]{2,1,0:T(8,128)S(1)} %broadcast_select_fusion, pred[8,132,132]{2,1,0:T(8,128)(4,1)S(1)} %get-tuple-element.13, f32[8,132,132]{2,1,0:T(8,128)S(1)} %get-tuple-element.4, f32[8,132,132]{2,1,0:T(8,128)S(1)} %get-tuple-element.12, ...), kind=kLoop, calls=%fused_computation.54 | loop fusion | flops 1926600 | bytes 7402200 | tf_op jit(solution)/shard_map/jit(_where)/select_n | solution.py:211
  138.6 2.0 %fusion.35 = f32[4,128,128]{2,1,0:T(8,128)} fusion(f32[8,132,132]{2,1,0:T(8,128)S(1)} %broadcast_select_fusion, f32[6,130,130]{2,1,0:T(8,128)S(1)} %get-tuple-element.2, f32[8,132,132]{2,1,0:T(8,128)S(1)} %get-tuple-element.12, f32[8,132,132]{2,1,0:T(8,128)S(1)} %get-tuple-element.11, f32[8,132,132]{2,1,0:T(8,128)S(1)} %get-tuple-element.10, ...), kind=kLoop, calls=%fused_computation.77 | loop fusion | flops 1441792 | bytes 5046272 | tf_op jit(solution)/shard_map/add | solution.py:199
  (79 shorter events, 29.4 us)
Async XLA Ops:
  0.6 37.8 %copy-start = (bf16[1,64,4096]{2,1,0:T(8,128)(2,1)S(1)}, bf16[1,64,4096]{2,1,0:T(8,128)(2,1)}, u32[]{:S(2)}) copy-start(bf16[1,64,4096]{2,1,0:T(8,128)(2,1)} %param.13) | copy-start | bytes 1572868
  0.6 24.6 %copy-start.10 = (s32[1,64]{1,0:T(1,128)S(1)}, s32[1,64]{1,0:T(1,128)}, u32[]{:S(2)}) copy-start(s32[1,64]{1,0:T(1,128)} %param.17) | copy-start | bytes 772
  0.7 33.2 %copy-start.9 = (f32[1,16]{1,0:T(1,128)S(1)}, f32[1,16]{1,0:T(1,128)}, u32[]{:S(2)}) copy-start(f32[1,16]{1,0:T(1,128)} %param.19) | copy-start | bytes 196
  5.4 15.6 %all-to-all-start = ((bf16[16,1,4]{2,1,0:T(2,128)(2,1)}), bf16[16,1,4]{2,1,0:T(2,128)(2,1)S(1)}, u32[]{:S(2)}, u32[]{:S(2)}) async-start(bf16[16,1,4]{2,1,0:T(2,128)(2,1)} %all_to_all.32), calls=%async_computation | async-start | bytes 16384 | tf_op jit(solution)/shard_map/all_to_all | solution.py:134
  21.8 10.7 %all-to-all-start.2 = ((f32[16,1,4]{2,1,0:T(1,128)}), f32[16,1,4]{2,1,0:T(1,128)S(1)}, u32[]{:S(2)}, u32[]{:S(2)}) async-start(f32[16,1,4]{2,1,0:T(1,128)} %bitcast.35), calls=%async_computation.2 | async-start | bytes 16384 | tf_op jit(solution)/shard_map/all_to_all | solution.py:140
  35.0 10.7 %all-to-all-start.3 = ((f32[16,1,4]{2,1,0:T(1,128)}), f32[16,1,4]{2,1,0:T(1,128)S(1)}, u32[]{:S(2)}, u32[]{:S(2)}) async-start(f32[16,1,4]{2,1,0:T(1,128)} %bitcast.23), calls=%async_computation.3 | async-start | bytes 16384 | tf_op jit(solution)/shard_map/all_to_all | solution.py:146
  38.8 10.5 %copy-start.6 = (bf16[1,64,4096]{2,1,0:T(8,128)(2,1)S(1)}, bf16[1,64,4096]{2,1,0:T(8,128)(2,1)}, u32[]{:S(2)}) copy-start(bf16[1,64,4096]{2,1,0:T(8,128)(2,1)} %param.14) | copy-start | bytes 1572868
  45.6 16.3 %all-to-all-start.1 = ((bf16[16,4,4096]{2,1,0:T(4,128)(2,1)}), bf16[16,4,4096]{2,1,0:T(4,128)(2,1)S(1)}, u32[]{:S(2)}, u32[]{:S(2)}) async-start(bf16[16,4,4096]{2,1,0:T(4,128)(2,1)} %reshape.105), calls=%async_computation.1 | async-start | bytes 1048576 | tf_op jit(solution)/shard_map/all_to_all | solution.py:132
  61.9 17.3 %all-to-all-start.4 = ((bf16[16,4,4096]{2,1,0:T(4,128)(2,1)}), bf16[16,4,4096]{2,1,0:T(4,128)(2,1)S(1)}, u32[]{:S(2)}, u32[]{:S(2)}) async-start(bf16[16,4,4096]{2,1,0:T(4,128)(2,1)} %reshape.108), calls=%async_computation.4 | async-start | bytes 1048576 | tf_op jit(solution)/shard_map/all_to_all | solution.py:133
  80.9 1.0 copy-start.1
  80.9 1.1 copy-start.3
  80.9 1.1 copy-start.4
  81.4 10.2 %copy-start.2 = (f32[4,2,64,2,64]{4,3,2,1,0:T(2,128)}, f32[4,2,64,2,64]{4,3,2,1,0:T(2,128)S(1)}, u32[]{:S(2)}) copy-start(f32[4,2,64,2,64]{4,3,2,1,0:T(2,128)S(1)} %copy.47) | copy-start | bytes 786436
  82.1 3.5 %collective-permute-start = (f32[4,4,3,128]{3,2,1,0:T(4,128)S(1)}, f32[4,4,3,128]{3,2,1,0:T(4,128)}, u32[]{:S(2)}, u32[]{:S(2)}) collective-permute-start(f32[4,4,3,128]{3,2,1,0:T(4,128)S(1)} %get-tuple-element.22), channel_id=1, source_target_pairs={{0,8},{8,16},{16,24},{1,9},{9,17},{17,25},{2,10},{10,18},{18,26},{... | collective-permute-start | bytes 73736 | tf_op jit(solution)/shard_map/ppermute | solution.py:23
  84.2 5.8 %collective-permute-start.1 = (f32[4,4,3,128]{3,2,1,0:T(4,128)S(1)}, f32[4,4,3,128]{3,2,1,0:T(4,128)S(1)}, u32[]{:S(2)}, u32[]{:S(2)}) collective-permute-start(f32[4,4,3,128]{3,2,1,0:T(4,128)S(1)} %get-tuple-element.23), channel_id=1, source_target_pairs={{8,0},{16,8},{24,16},{9,1},{17,9},{25,17},{10,2},{18,10},{26,18},{... | collective-permute-start | bytes 73736 | tf_op jit(solution)/shard_map/ppermute | solution.py:25
  90.0 0.6 copy-start.7
  94.8 4.6 %collective-permute-start.2 = (f32[4,4,134,3]{2,1,3,0:T(4,128)S(1)}, f32[4,4,134,3]{2,1,3,0:T(4,128)S(1)}, u32[]{:S(2)}, u32[]{:S(2)}) collective-permute-start(f32[4,4,134,3]{2,1,3,0:T(4,128)S(1)} %copy.48), channel_id=1, source_target_pairs={{0,2},{2,4},{4,6},{1,3},{3,5},{5,7},{8,10},{10,12},{12,14},{9,11},... | collective-permute-start | bytes 77192 | tf_op jit(solution)/shard_map/ppermute | solution.py:23
  98.0 6.1 %collective-permute-start.3 = (f32[4,4,134,3]{2,1,3,0:T(4,128)S(1)}, f32[4,4,134,3]{2,1,3,0:T(4,128)}, u32[]{:S(2)}, u32[]{:S(2)}) collective-permute-start(f32[4,4,134,3]{2,1,3,0:T(4,128)S(1)} %copy.49), channel_id=1, source_target_pairs={{2,0},{4,2},{6,4},{3,1},{5,3},{7,5},{10,8},{12,10},{14,12},{11,9},... | collective-permute-start | bytes 77192 | tf_op jit(solution)/shard_map/ppermute | solution.py:25
  109.5 10.5 %collective-permute-start.5 = (f32[4,3,134,134]{3,0,2,1:T(4,128)}, f32[4,3,134,134]{3,0,2,1:T(4,128)}, u32[]{:S(2)}, u32[]{:S(2)}) collective-permute-start(f32[4,3,134,134]{3,0,2,1:T(4,128)} %copy.53), channel_id=1, source_target_pairs={{1,0},{3,2},{5,4},{7,6},{9,8},{11,10},{13,12},{15,14},{17,16},{19,... | collective-permute-start | bytes 2585672 | tf_op jit(solution)/shard_map/ppermute | solution.py:25
  112.6 9.2 %collective-permute-start.4 = (f32[4,3,134,134]{3,0,2,1:T(4,128)}, f32[4,3,134,134]{3,0,2,1:T(4,128)}, u32[]{:S(2)}, u32[]{:S(2)}) collective-permute-start(f32[4,3,134,134]{3,0,2,1:T(4,128)} %copy.52), channel_id=1, source_target_pairs={{0,1},{2,3},{4,5},{6,7},{8,9},{10,11},{12,13},{14,15},{16,17},{18,... | collective-permute-start | bytes 2585672 | tf_op jit(solution)/shard_map/ppermute | solution.py:23
  121.8 1.8 %copy-start.5 = (f32[4,128,128]{2,1,0:T(8,128)S(1)}, f32[4,128,128]{2,1,0:T(8,128)}, u32[]{:S(2)}) copy-start(f32[4,128,128]{2,1,0:T(8,128)} %param.11) | copy-start | bytes 786436
  121.8 1.8 %copy-start.8 = (f32[4,4,3,128]{3,2,1,0:T(4,128)S(1)}, f32[4,4,3,128]{3,2,1,0:T(4,128)}, u32[]{:S(2)}) copy-start(f32[4,4,3,128]{3,2,1,0:T(4,128)} %copy-done.7) | copy-start | bytes 73732
where the time goes:
time: 142 us; the launch traced here: 141 us
  waiting for transfers between devices  51.5 us (36%)
  starting transfers between devices  36.5 us (26%)
  other arithmetic  25.3 us (18%)
  local copies, waits for them, and re-layouts  23.3 us (16%)
  matrix products  2.8 us (2%)
    all_to_all x1, waiting for transfers between devices, shards(): lax.all_to_all(leak_send, ('row', 'col'), split_axis=0, concat_axis=0, ti...  12.8 us
    all_to_all x1, waiting for transfers between devices, shards(): lax.all_to_all(dyn_send, ('row', 'col'), split_axis=0, concat_axis=0, til...  11.4 us
    ppermute x3, starting transfers between devices, padded_2(): lax.ppermute(tail, axis, [(i, (i + 1) % count) for i in range(ends)])  10.2 us
    concatenate x3, other arithmetic, padded_2(): jnp.concatenate([lax.ppermute(tail, axis, [(i, (i + 1) % count) for i in...  8.97 us
    ppermute x3, waiting for transfers between devices, padded_2(): lax.ppermute(head, axis, [((i + 1) % count, i) for i in range(ends)])  8.85 us
    all_to_all x1, starting transfers between devices, shards(): lax.all_to_all(place_send, ('row', 'col'), split_axis=0, concat_axis=0, t...  8.34 us
    all_to_all x1, waiting for transfers between devices, shards(): lax.all_to_all(means_there, ('row', 'col'), split_axis=0, concat_axis=0,...  7.08 us
    all_to_all x1, waiting for transfers between devices, shards(): lax.all_to_all(factor_send, ('row', 'col'), split_axis=0, concat_axis=0,...  5.89 us
  transfers between devices with their start and end apart: 11, of which 7 were waited for; matrix products, arithmetic and copies ran while one was open for 8% of the time, Pallas kernels for 0%

commit v1 on v0

v1 whole, which is shorter than its diff:
```python
import functools
import jax
import jax.numpy as jnp
from jax import lax
from jax.experimental import pallas as pl
from jax.experimental.pallas import tpu as pltpu
from jax.sharding import PartitionSpec as P

SUB = 64
SWEEPS = 3
CAP = 4
EIG_LOW = 0.1
EIG_HIGH = 2.0
LANES = 128
PACK = 16

MESH = pl.DeviceIdType.MESH
F32 = jnp.float32
BF16 = jnp.bfloat16


def iota(shape, dim):
    return lax.broadcasted_iota(jnp.int32, shape, dim)


def hi_dot(a, b, dims):
    return lax.dot_general(
        a, b, (dims, ((), ())), precision=lax.Precision.HIGHEST, preferred_element_type=F32
    )


def kernel(
    sizes,
    temp_hbm,
    cond_hbm,
    mass_hbm,
    dyn_hbm,
    leak_hbm,
    panel_ref,
    place_ref,
    block_ref,
    tier_ref,
    sens_ref,
    out_ref,
    power_ref,
    temp,
    cond,
    mass,
    dyn,
    leak,
    note_send,
    note_recv,
    load_send,
    load_recv,
    dirs,
    faces,
    diag,
    inv,
    resid,
    edge_send,
    edge_recv,
    plane_recv,
    in_sem,
    note_ssem,
    note_rsem,
    load_ssem,
    load_rsem,
    halo_ssem,
    halo_rsem,
):
    n_row, n_col, n_layer = sizes
    tiles = n_row * n_col
    tiers, rows, cols = temp.shape
    slots, cells = dyn.shape
    folds = PACK // CAP
    wide = cells // folds
    note_rows = note_send.shape[0] // tiles
    in_plane = (rows // SUB) * (cols // SUB)
    patches = tiers * in_plane
    bands = tiers * (rows // SUB)
    chunks = tiles * PACK // LANES

    my_row = lax.axis_index("row")
    my_col = lax.axis_index("col")
    my_layer = lax.axis_index("layer")
    me = my_row * n_col + my_col

    loads = [
        pltpu.make_async_copy(src, dst, in_sem.at[i])
        for i, (src, dst) in enumerate(
            (
                (temp_hbm, temp),
                (cond_hbm, cond),
                (dyn_hbm.at[0], dyn),
                (leak_hbm.at[0], leak),
                (mass_hbm, mass),
            )
        )
    ]
    for load in loads:
        load.start()

    def peer(step):
        other = lax.rem(me + step, tiles)
        return other, {"row": other // n_col, "col": lax.rem(other, n_col)}

    sides = (
        (my_layer > 0, {"layer": my_layer - 1}, 0),
        (my_layer < n_layer - 1, {"layer": my_layer + 1}, 1),
        (my_row > 0, {"row": my_row - 1}, 2),
        (my_row < n_row - 1, {"row": my_row + 1}, 3),
        (my_col > 0, {"col": my_col - 1}, 4),
        (my_col < n_col - 1, {"col": my_col + 1}, 5),
    )

    barrier = pltpu.get_barrier_semaphore()

    @pl.loop(1, tiles)
    def _(step):
        _, where = peer(step)
        pl.semaphore_signal(barrier, inc=1, device_id=where, device_id_type=MESH)

    for exists, where, side in sides[:2]:

        @pl.when(exists)
        def _(where=where):
            pl.semaphore_signal(barrier, inc=1, device_id=where, device_id_type=MESH)

    for turn in range(4):
        for exists, _, side in sides:

            @pl.when(jnp.logical_not(exists))
            def _(turn=turn, side=side):
                if side < 2:
                    plane_recv[turn, side] = jnp.zeros((rows, cols), F32)
                else:
                    edge_recv[turn, side - 2] = jnp.zeros(edge_recv.shape[2:], F32)

    lane_s = iota((slots, slots), 1)
    sub_s = iota((slots, slots), 0)
    eye = lane_s == sub_s

    def to_col(row):
        return jnp.sum(jnp.where(eye, jnp.broadcast_to(row, (slots, slots)), 0.0), axis=1, keepdims=True)

    def to_row(col):
        return jnp.sum(jnp.where(eye, jnp.broadcast_to(col, (slots, slots)), 0.0), axis=0, keepdims=True)

    tgt_col = panel_ref[...].astype(F32)
    tgt_row = to_row(tgt_col)
    blk_row = block_ref[...].astype(F32)
    blk_col = to_col(blk_row)
    sub_col = to_col(place_ref[...].astype(F32))
    same_tile = tgt_col == tgt_row
    rank_col = jnp.sum(jnp.where(same_tile & (lane_s < sub_s), 1.0, 0.0), axis=1, keepdims=True)
    rank_row = jnp.sum(jnp.where(same_tile & (sub_s < lane_s), 1.0, 0.0), axis=0, keepdims=True)
    blocks = tier_ref.shape[1]
    of_block = blk_col == iota((slots, blocks), 1).astype(F32)
    tier_col = jnp.sum(jnp.where(of_block, tier_ref[...].astype(F32), 0.0), axis=1, keepdims=True)
    sens_col = jnp.sum(jnp.where(of_block, sens_ref[...], 0.0), axis=1, keepdims=True)
    pos_col = tier_col * in_plane + sub_col
    same_block = jnp.where(blk_col == blk_row, 1.0, 0.0)
    block_size = jnp.sum(same_block, axis=1, keepdims=True)

    offset = lax.rem(me * PACK, LANES)
    my_chunk = (me * PACK) // LANES
    rel = iota((slots, LANES), 1) - offset
    fits = (rel >= 0) & (rel < PACK) & ((rel & (CAP - 1)).astype(F32) == rank_col)
    place_lanes = jnp.where(fits, pos_col + 1.0, 0.0)
    note_i = iota((tiles * note_rows, slots), 0)
    to_tile = jnp.where(
        ((note_i // note_rows).astype(F32) == tgt_row) & (lax.rem(note_i, note_rows) == 1 + my_chunk),
        1.0,
        0.0,
    )
    places = jnp.dot(to_tile.astype(BF16), place_lanes.astype(BF16), preferred_element_type=F32)

    loads[0].wait()
    band_sums = jnp.concatenate(
        [
            jnp.sum(temp[t, b * SUB : (b + 1) * SUB, :], axis=0, keepdims=True)
            for t in range(tiers)
            for b in range(rows // SUB)
        ],
        axis=0,
    )
    lane_b = iota((bands, LANES), 1)
    sub_b = iota((bands, LANES), 0)
    means = jnp.zeros((1, LANES), F32)
    per_band = cols // SUB
    for part in range(per_band):
        total = jnp.sum(jnp.where(lane_b // SUB == part, band_sums, 0.0), axis=1, keepdims=True)
        means = means + jnp.sum(
            jnp.where(lane_b == sub_b * per_band + part, total, 0.0), axis=0, keepdims=True
        )
    means = means * (1.0 / (SUB * SUB))
    note_j = iota((tiles * note_rows, LANES), 0)
    note_send[...] = places + jnp.where(lax.rem(note_j, note_rows) == 0, means, 0.0)

    sub8 = iota((2 * tiers, LANES), 0)
    lane8 = iota((2 * tiers, LANES), 1)

    def halo_copy(turn, field, where, side, lands):
        if side < 2:
            src = field.at[0 if side == 0 else tiers - 1]
            dst = plane_recv.at[turn, lands]
        else:
            src = edge_send.at[turn, (side - 2) // 2]
            dst = edge_recv.at[turn, lands - 2]
        return pltpu.make_async_remote_copy(
            src_ref=src,
            dst_ref=dst,
            send_sem=halo_ssem.at[turn, side],
            recv_sem=halo_rsem.at[turn, lands],
            device_id=where,
            device_id_type=MESH,
        )

    def pack_edges(turn, field):
        for end in range(2):
            at = end * (rows - 1)
            for t in range(tiers):
                edge_send[turn, 0, end * tiers + t : end * tiers + t + 1, :] = field[t, at : at + 1, :]
        columns = jnp.zeros((2 * tiers, rows), F32)
        for t in range(tiers):
            pick = jnp.where(
                ((sub8 == t) & (lane8 == 0)) | ((sub8 == tiers + t) & (lane8 == cols - 1)), 1.0, 0.0
            )
            columns = columns + hi_dot(pick, field[t], ((1,), (1,)))
        edge_send[turn, 1] = columns

    def each_side(act):
        for exists, where, side in sides:
            pl.when(exists)(functools.partial(act, where, side))

    def start_halo(turn, field):
        each_side(lambda where, side: halo_copy(turn, field, where, side, side ^ 1).start())

    def wait_halo(turn, field):
        each_side(lambda where, side: halo_copy(turn, field, where, side, side).wait_recv())

    def end_halo(turn, field):
        each_side(lambda where, side: halo_copy(turn, field, where, side, side ^ 1).wait_send())

    row_i = iota((rows, cols), 0)
    col_i = iota((rows, cols), 1)

    def beside(turn, field):
        ends = jnp.concatenate([edge_recv[turn, 2], edge_recv[turn, 3]], axis=0)
        sub16 = iota((4 * tiers, LANES), 0)
        lane16 = iota((4 * tiers, LANES), 1)
        result = []
        for t in range(tiers):
            v = field[t]
            low = plane_recv[turn, 0] if t == 0 else field[t - 1]
            high = plane_recv[turn, 1] if t == tiers - 1 else field[t + 1]
            north = jnp.where(
                row_i == 0, edge_recv[turn, 0, tiers + t : tiers + t + 1, :], pltpu.roll(v, 1, 0)
            )
            south = jnp.where(
                row_i == rows - 1, edge_recv[turn, 1, t : t + 1, :], pltpu.roll(v, rows - 1, 0)
            )
            put = jnp.where(
                ((sub16 == tiers + t) & (lane16 == 0))
                | ((sub16 == 2 * tiers + t) & (lane16 == cols - 1)),
                1.0,
                0.0,
            )
            rim = hi_dot(ends, put, ((0,), (0,)))
            west = jnp.where(col_i == 0, rim, pltpu.roll(v, 1, 1))
            east = jnp.where(col_i == cols - 1, rim, pltpu.roll(v, cols - 1, 1))
            result.append((v, (low, high, north, south, west, east)))
        return result

    beyond = (my_layer > 0).astype(jnp.int32) + (my_layer < n_layer - 1).astype(jnp.int32)
    pl.semaphore_wait(barrier, tiles - 1 + beyond)

    def note_copy(step):
        other, where = peer(step)
        return pltpu.make_async_remote_copy(
            src_ref=note_send.at[pl.ds(other * note_rows, note_rows), :],
            dst_ref=note_recv.at[pl.ds(me * note_rows, note_rows), :],
            send_sem=note_ssem.at[step],
            recv_sem=note_rsem.at[step],
            device_id=where,
            device_id_type=MESH,
        )

    def load_copy(step):
        other, where = peer(step)
        return pltpu.make_async_remote_copy(
            src_ref=load_send.at[pl.ds(other * PACK, PACK), :],
            dst_ref=load_recv.at[pl.ds(me * PACK, PACK), :],
            send_sem=load_ssem.at[step],
            recv_sem=load_rsem.at[step],
            device_id=where,
            device_id_type=MESH,
        )

    @pl.loop(1, tiles)
    def _(step):
        note_copy(step).start()

    own_note = pl.ds(pl.multiple_of(me * note_rows, note_rows), note_rows)
    own_copy = pltpu.make_async_copy(note_send.at[own_note, :], note_recv.at[own_note, :], note_rsem.at[0])
    own_copy.start()

    loads[1].wait()
    pack_edges(0, temp)
    start_halo(0, temp)
    pack_edges(1, cond)
    start_halo(1, cond)
    loads[2].wait()
    loads[3].wait()
    own_copy.wait()

    @pl.loop(1, tiles)
    def _(step):
        note_copy(step).wait_recv()

    note_k = iota((slots, tiles * note_rows), 1)
    from_tile = jnp.where(
        ((note_k // note_rows).astype(F32) == tgt_col) & (lax.rem(note_k, note_rows) == 0), 1.0, 0.0
    )
    tile_means = hi_dot(from_tile, note_recv[...], ((1,), (0,)))
    slot_mean = jnp.sum(
        jnp.where(iota((slots, LANES), 1).astype(F32) == pos_col, tile_means, 0.0), axis=1, keepdims=True
    )
    block_rise = jnp.sum(same_block * to_row(slot_mean), axis=1, keepdims=True) / block_size
    factor = jnp.exp(sens_col * block_rise)
    send_i = iota((tiles * PACK, slots), 0)
    goes = (
        (send_i // PACK) * CAP + lax.rem(send_i, CAP)
    ).astype(F32) == tgt_row * CAP + rank_row
    fold_i = lax.rem(send_i, PACK) // CAP
    gathered = jnp.zeros((tiles * PACK, wide), F32)
    for fold in range(folds):
        part = slice(fold * wide, (fold + 1) * wide)
        slot_power = (dyn[:, part].astype(F32) + factor * leak[:, part].astype(F32)).astype(BF16)
        pick = jnp.where(goes & (fold_i == fold), 1.0, 0.0).astype(BF16)
        gathered = gathered + jnp.dot(pick, slot_power, preferred_element_type=F32)
    load_send[...] = gathered.astype(BF16)

    @pl.loop(1, tiles)
    def _(step):
        load_copy(step).start()

    own_load = pl.ds(pl.multiple_of(me * PACK, PACK), PACK)
    own_move = pltpu.make_async_copy(load_send.at[own_load, :], load_recv.at[own_load, :], load_rsem.at[0])
    own_move.start()

    loads[4].wait()
    wait_halo(0, temp)
    wait_halo(1, cond)
    near = beside(1, cond)
    for t in range(tiers):
        c, around = near[t]
        total = mass[t]
        for k in range(6):
            face = 0.5 * (c + around[k])
            faces[k, t] = face
            total = total + face
        diag[t] = total
        inv[t] = 1.0 / total
    near = beside(0, temp)
    for t in range(tiers):
        v, around = near[t]
        value = diag[t] * v
        for k in range(6):
            value = value - faces[k, t] * around[k]
        resid[t] = mass[t] * v - value

    middle = (EIG_LOW + EIG_HIGH) / 2.0
    spread = (EIG_HIGH - EIG_LOW) / 2.0
    ratio = middle / spread
    weight = 1.0 / ratio

    sel_i = iota((folds * patches, LANES), 0)
    sel_j = iota((folds * patches, LANES), 1)
    sel_fold = sel_i // patches
    sel_in = lax.rem(sel_i, patches)
    sel_patch = lax.rem(sel_in, bands) * per_band + sel_in // bands
    fold_hit = sel_fold == lax.rem(sel_j, PACK) // CAP
    notes = note_recv[...]
    pickers = []
    for chunk in range(chunks):
        code = jnp.sum(jnp.where(lax.rem(note_j, note_rows) == 1 + chunk, notes, 0.0), axis=0, keepdims=True)
        pickers.append(
            jnp.where(fold_hit & (code == (sel_patch + 1).astype(F32)), 1.0, 0.0).astype(BF16)
        )

    own_move.wait()

    @pl.loop(1, tiles)
    def _(step):
        load_copy(step).wait_recv()

    footprint = jnp.zeros((folds * patches, wide), F32)
    for chunk in range(chunks):
        footprint = footprint + jnp.dot(
            pickers[chunk], load_recv[chunk * LANES : (chunk + 1) * LANES, :], preferred_element_type=F32
        )
    left = iota((bands, LANES), 1) < SUB
    for fold in range(folds):
        for k in range(wide // LANES):
            lanes = slice(k * LANES, (k + 1) * LANES)
            a = footprint[fold * patches : fold * patches + bands, lanes]
            b = footprint[fold * patches + bands : fold * patches + 2 * bands, lanes]
            at = 2 * (fold * (wide // LANES) + k)
            power_ref[pl.ds(at, bands, stride=SUB), :] = jnp.where(left, a, pltpu.roll(b, SUB, 1))
            power_ref[pl.ds(at + 1, bands, stride=SUB), :] = jnp.where(left, pltpu.roll(a, SUB, 1), b)

    for t in range(tiers):
        r = resid[t] + power_ref[t * rows : (t + 1) * rows, :]
        resid[t] = r
        dirs[0, t] = r * inv[t] * (1.0 / middle)
    for sweep in range(1, SWEEPS):
        field = dirs.at[sweep - 1]
        turn = 1 + sweep
        pack_edges(turn, field)
        start_halo(turn, field)
        for t in range(tiers):
            base = temp[t] if sweep == 1 else out_ref[t]
            out_ref[t] = base + field[t]
        wait_halo(turn, field)
        weight_new = 1.0 / (2.0 * ratio - weight)
        near = beside(turn, field)
        for t in range(tiers):
            v, around = near[t]
            value = diag[t] * v
            for k in range(6):
                value = value - faces[k, t] * around[k]
            r = resid[t] - value
            if sweep < SWEEPS - 1:
                resid[t] = r
            d = weight_new * weight * v + (2.0 * weight_new / spread) * (r * inv[t])
            if sweep < SWEEPS - 1:
                dirs[sweep, t] = d
            else:
                out_ref[t] = out_ref[t] + d
        weight = weight_new

    end_halo(0, temp)
    end_halo(1, cond)
    for sweep in range(1, SWEEPS):
        end_halo(1 + sweep, dirs.at[sweep - 1])

    @pl.loop(1, tiles)
    def _(step):
        note_copy(step).wait_send()
        load_copy(step).wait_send()


def shards(sizes, temp, cond, mass, dyn, leak, panel, place, block, tier, sens):
    tiers, rows, cols = temp.shape
    slots, cells = dyn.shape[1:]
    tiles = sizes[0] * sizes[1]
    folds = PACK // CAP
    note_rows = -(-(1 + tiles * PACK // LANES) // 8) * 8
    any_spec = pl.BlockSpec(memory_space=pl.ANY)
    vmem = pl.BlockSpec(memory_space=pltpu.VMEM)
    grid = (tiers, rows, cols)
    dma = pltpu.SemaphoreType.DMA
    new, power = pl.pallas_call(
        functools.partial(kernel, sizes),
        out_shape=(
            jax.ShapeDtypeStruct(grid, F32),
            jax.ShapeDtypeStruct((tiers * rows, cols), F32),
        ),
        in_specs=[any_spec] * 5 + [vmem] * 5,
        out_specs=(vmem, vmem),
        scratch_shapes=[
            pltpu.VMEM(grid, F32),
            pltpu.VMEM(grid, F32),
            pltpu.VMEM(grid, F32),
            pltpu.VMEM((slots, cells), BF16),
            pltpu.VMEM((slots, cells), BF16),
            pltpu.VMEM((tiles * note_rows, LANES), F32),
            pltpu.VMEM((tiles * note_rows, LANES), F32),
            pltpu.VMEM((tiles * PACK, cells // folds), BF16),
            pltpu.VMEM((tiles * PACK, cells // folds), BF16),
            pltpu.VMEM((SWEEPS - 1,) + grid, F32),
            pltpu.VMEM((6,) + grid, F32),
            pltpu.VMEM(grid, F32),
            pltpu.VMEM(grid, F32),
            pltpu.VMEM(grid, F32),
            pltpu.VMEM((SWEEPS + 1, 2, 2 * tiers, cols), F32),
            pltpu.VMEM((SWEEPS + 1, 4, 2 * tiers, cols), F32),
            pltpu.VMEM((SWEEPS + 1, 2, rows, cols), F32),
            dma((5,)),
            dma((tiles,)),
            dma((tiles,)),
            dma((tiles,)),
            dma((tiles,)),
            dma((SWEEPS + 1, 6)),
            dma((SWEEPS + 1, 6)),
        ],
        compiler_params=pltpu.CompilerParams(
            collective_id=0, has_side_effects=True, vmem_limit_bytes=48 * 1024 * 1024
        ),
    )(temp, cond, mass, dyn, leak, panel[0], place, block, tier, sens)
    return new, power.reshape(grid)


def solution(mesh):
    sizes = (mesh.shape["row"], mesh.shape["col"], mesh.shape["layer"])
    owner = ("row", "col", "layer")
    return jax.shard_map(
        functools.partial(shards, sizes),
        mesh=mesh,
        in_specs=(P("layer", "row", "col"),) * 3
        + (P(owner, None, None),) * 3
        + (P(owner, None),) * 4,
        out_specs=(P("layer", "row", "col"), P("layer", "row", "col")),
        check_vma=False,
    )
```

time: 142 us -> 43.5 us (0.31)
  waiting for transfers between devices: 51.5 us -> 0 us
  starting transfers between devices: 36.5 us -> 0 us
  Pallas kernels: 0 us -> 34.8 us
  other arithmetic: 25.3 us -> 0 us
  local copies, waits for them, and re-layouts: 23.3 us -> 7.68 us
  matrix products: 2.8 us -> 0 us
    all_to_all x5 -> x0, waiting for transfers between devices: 42.7 us -> none  [the longest x1 12.8 us: shards(): lax.all_to_all(leak_send, ('row', 'col'), split_axis=0, concat_axis=0, ti...]
    pallas_call x0 -> x1, Pallas kernels: none -> 34.8 us  [shards(): pl.pallas_call(functools.partial(kernel, sizes), out_shape=(jax.ShapeDtyp...]
    all_to_all x5 -> x0, starting transfers between devices: 22.4 us -> none  [the longest x1 8.34 us: shards(): lax.all_to_all(place_send, ('row', 'col'), split_axis=0, concat_axis=0, t...]
    ppermute x6 -> x0, starting transfers between devices: 14.1 us -> none  [the longest x3 10.2 us: padded_2(): lax.ppermute(tail, axis, [(i, (i + 1) % count) for i in range(ends)])]
    concatenate x3 -> x0, other arithmetic: 8.97 us -> none  [padded_2(): jnp.concatenate([lax.ppermute(tail, axis, [(i, (i + 1) % count) for i in...]
    ppermute x6 -> x0, waiting for transfers between devices: 8.86 us -> none  [the longest x3 8.85 us: padded_2(): lax.ppermute(head, axis, [((i + 1) % count, i) for i in range(ends)])]
    select_n x3 -> x0, other arithmetic: 8.39 us -> none  [the longest x1 4.64 us: shards(): jnp.where(inside, remaining_imbalance / (safe_diag * middle), 0.0)]
    slice x6 -> x0, local copies, waits for them, and re-layouts: 7.77 us -> none  [the longest x4 5.33 us: padded_2(): lax.slice_in_dim(cells, cells.shape[dim] - width, cells.shape[dim], axis=...]
  transfers between devices with their start and end apart: 11 -> 0, of which waited for: 7 -> 0; matrix products, arithmetic and copies ran while one was open for 8% -> 0% of each run, Pallas kernels for 0% -> 0%
where the time goes in v1:
time: 43.5 us; the launch traced here: 43.1 us
  Pallas kernels  34.8 us (80%)
  local copies, waits for them, and re-layouts  7.68 us (18%)
  between operations  0.66 us (2%)
    pallas_call x1, Pallas kernels, shards(): pl.pallas_call(functools.partial(kernel, sizes), out_shape=(jax.ShapeDtyp...  34.8 us
    unnamed x22, local copies, waits for them, and re-layouts  7.59 us

profile of v1, /device:TPU:0, one launch (start us, length us, event | category | flops | bytes accessed | tf_op | source)
XLA Modules:
  0.0 43.1 jit_solution(16764932383195648401)
XLA Ops:
  0.6 0.0 copy-start.9
  0.6 0.6 %copy-done.9 = s32[1,64,1]{1,2,0:T(1,128)S(1)} copy-done((s32[1,64,1]{1,2,0:T(1,128)S(1)}, s32[1,64,1]{1,2,0:T(1,128)}, u32[]{:S(2)}) %copy-start.9) | copy-done | bytes 280
  1.3 0.0 copy-start.5
  1.3 0.0 copy-start.6
  1.3 0.0 copy-start.7
  1.3 0.0 copy-start.8
  1.3 0.1 copy.12.panel_ref
  1.4 0.5 %copy-done.5 = s32[1,64]{1,0:T(1,128)S(1)} copy-done((s32[1,64]{1,0:T(1,128)S(1)}, s32[1,64]{1,0:T(1,128)}, u32[]{:S(2)}) %copy-start.5) | copy-done | bytes 280
  1.9 0.0 copy-done.6
  2.0 0.0 copy-done.7
  2.0 0.0 copy-done.8
  2.0 0.0 copy-start
  2.0 1.0 %copy-done = bf16[1,64,4096]{2,1,0:T(8,128)(2,1)S(1)} copy-done((bf16[1,64,4096]{2,1,0:T(8,128)(2,1)S(1)}, bf16[1,64,4096]{2,1,0:T(8,128)(2,1)}, u32[]{:S(2)}) %copy-start) | copy-done | bytes 524312
  3.0 0.0 copy-start.1
  3.0 1.0 %copy-done.1 = bf16[1,64,4096]{2,1,0:T(8,128)(2,1)S(1)} copy-done((bf16[1,64,4096]{2,1,0:T(8,128)(2,1)S(1)}, bf16[1,64,4096]{2,1,0:T(8,128)(2,1)}, u32[]{:S(2)}) %copy-start.1) | copy-done | bytes 524312
  4.1 0.0 copy-start.2
  4.1 0.9 %copy-done.2 = f32[4,128,128]{2,1,0:T(8,128)S(1)} copy-done((f32[4,128,128]{2,1,0:T(8,128)S(1)}, f32[4,128,128]{2,1,0:T(8,128)}, u32[]{:S(2)}) %copy-start.2) | copy-done | bytes 262168
  5.0 0.0 copy-start.3
  5.0 0.9 %copy-done.3 = f32[4,128,128]{2,1,0:T(8,128)S(1)} copy-done((f32[4,128,128]{2,1,0:T(8,128)S(1)}, f32[4,128,128]{2,1,0:T(8,128)}, u32[]{:S(2)}) %copy-start.3) | copy-done | bytes 262168
  6.0 0.0 copy-start.4
  6.0 0.9 %copy-done.4 = f32[4,128,128]{2,1,0:T(8,128)S(1)} copy-done((f32[4,128,128]{2,1,0:T(8,128)S(1)}, f32[4,128,128]{2,1,0:T(8,128)}, u32[]{:S(2)}) %copy-start.4) | copy-done | bytes 262168
  6.9 34.8 %shard_map.113 = (f32[4,128,128]{2,1,0:T(8,128)S(1)}, f32[512,128]{1,0:T(8,128)S(1)}) custom-call(f32[4,128,128]{2,1,0:T(8,128)S(1)} %copy-done.2, f32[4,128,128]{2,1,0:T(8,128)S(1)} %copy-done.3, f32[4,128,128]{2,1,0:T(8,128)S(1)} %copy-done.4, bf16[1,64,4096]{2,1,0:T(8,128)(2,1)S(1)} %copy-done, bf16[1,64,4096]{2,1,0:T(8,128)(2,1)S(1)} %copy-done.1, ...), custom_call_target="tpu_custom_call" | custom-call | tf_op jit(solution)/shard_map/pallas_call | solution.py:464
  41.7 0.7 %copy.15 = f32[4,128,128]{2,1,0:T(8,128)} copy(f32[4,128,128]{2,1,0:T(8,128)S(1)} %get-tuple-element.8) | data formatting | bytes 524288
  42.4 0.7 %copy.16 = f32[4,128,128]{2,1,0:T(8,128)} copy(f32[4,128,128]{2,1,0:T(8,128)S(1)} %bitcast.2) | data formatting | bytes 524288
Async XLA Ops:
  0.6 0.7 %copy-start.9 = (s32[1,64,1]{1,2,0:T(1,128)S(1)}, s32[1,64,1]{1,2,0:T(1,128)}, u32[]{:S(2)}) copy-start(s32[1,64,1]{1,2,0:T(1,128)} %param.15) | copy-start | bytes 772
  1.3 0.7 %copy-start.5 = (s32[1,64]{1,0:T(1,128)S(1)}, s32[1,64]{1,0:T(1,128)}, u32[]{:S(2)}) copy-start(s32[1,64]{1,0:T(1,128)} %place_ref.1) | copy-start | bytes 772
  1.3 0.7 %copy-start.6 = (s32[1,64]{1,0:T(1,128)S(1)}, s32[1,64]{1,0:T(1,128)}, u32[]{:S(2)}) copy-start(s32[1,64]{1,0:T(1,128)} %block_ref.1) | copy-start | bytes 772
  1.3 0.7 %copy-start.7 = (s32[1,16]{1,0:T(1,128)S(1)}, s32[1,16]{1,0:T(1,128)}, u32[]{:S(2)}) copy-start(s32[1,16]{1,0:T(1,128)} %tier_ref.1) | copy-start | bytes 196
  1.3 0.7 %copy-start.8 = (f32[1,16]{1,0:T(1,128)S(1)}, f32[1,16]{1,0:T(1,128)}, u32[]{:S(2)}) copy-start(f32[1,16]{1,0:T(1,128)} %sens_ref.1) | copy-start | bytes 196
  2.0 1.0 %copy-start = (bf16[1,64,4096]{2,1,0:T(8,128)(2,1)S(1)}, bf16[1,64,4096]{2,1,0:T(8,128)(2,1)}, u32[]{:S(2)}) copy-start(bf16[1,64,4096]{2,1,0:T(8,128)(2,1)} %dyn_hbm.1) | copy-start | bytes 1572868
  3.0 1.0 %copy-start.1 = (bf16[1,64,4096]{2,1,0:T(8,128)(2,1)S(1)}, bf16[1,64,4096]{2,1,0:T(8,128)(2,1)}, u32[]{:S(2)}) copy-start(bf16[1,64,4096]{2,1,0:T(8,128)(2,1)} %leak_hbm.1) | copy-start | bytes 1572868
  4.1 0.9 %copy-start.2 = (f32[4,128,128]{2,1,0:T(8,128)S(1)}, f32[4,128,128]{2,1,0:T(8,128)}, u32[]{:S(2)}) copy-start(f32[4,128,128]{2,1,0:T(8,128)} %temp_hbm.1) | copy-start | bytes 786436
  5.0 0.9 %copy-start.3 = (f32[4,128,128]{2,1,0:T(8,128)S(1)}, f32[4,128,128]{2,1,0:T(8,128)}, u32[]{:S(2)}) copy-start(f32[4,128,128]{2,1,0:T(8,128)} %cond_hbm.1) | copy-start | bytes 786436
  6.0 0.9 %copy-start.4 = (f32[4,128,128]{2,1,0:T(8,128)S(1)}, f32[4,128,128]{2,1,0:T(8,128)}, u32[]{:S(2)}) copy-start(f32[4,128,128]{2,1,0:T(8,128)} %mass_hbm.1) | copy-start | bytes 786436

commit v2 on v1

--- a/solution.py
+++ b/solution.py
@@ -13,6 +13,7 @@
 EIG_HIGH = 2.0
 LANES = 128
 PACK = 16
+VMEM_BYTES = 67043328
 
 MESH = pl.DeviceIdType.MESH
 F32 = jnp.float32
@@ -36,6 +37,13 @@
     mass_hbm,
     dyn_hbm,
     leak_hbm,
+    panel_hbm,
+    place_hbm,
+    block_hbm,
+    tier_hbm,
+    sens_hbm,
+    out_hbm,
+    power_hbm,
     panel_ref,
     place_ref,
     block_ref,
@@ -61,6 +69,7 @@
     edge_recv,
     plane_recv,
     in_sem,
+    out_sem,
     note_ssem,
     note_rsem,
     load_ssem,
@@ -89,6 +98,11 @@
         pltpu.make_async_copy(src, dst, in_sem.at[i])
         for i, (src, dst) in enumerate(
             (
+                (panel_hbm, panel_ref),
+                (place_hbm, place_ref),
+                (block_hbm, block_ref),
+                (tier_hbm, tier_ref),
+                (sens_hbm, sens_ref),
                 (temp_hbm, temp),
                 (cond_hbm, cond),
                 (dyn_hbm.at[0], dyn),
@@ -146,8 +160,10 @@
     def to_row(col):
         return jnp.sum(jnp.where(eye, jnp.broadcast_to(col, (slots, slots)), 0.0), axis=0, keepdims=True)
 
-    tgt_col = panel_ref[...].astype(F32)
-    tgt_row = to_row(tgt_col)
+    for load in loads[:5]:
+        load.wait()
+    tgt_row = panel_ref[...].astype(F32)
+    tgt_col = to_col(tgt_row)
     blk_row = block_ref[...].astype(F32)
     blk_col = to_col(blk_row)
     sub_col = to_col(place_ref[...].astype(F32))
@@ -175,7 +191,7 @@
     )
     places = jnp.dot(to_tile.astype(BF16), place_lanes.astype(BF16), preferred_element_type=F32)
 
-    loads[0].wait()
+    loads[5].wait()
     band_sums = jnp.concatenate(
         [
             jnp.sum(temp[t, b * SUB : (b + 1) * SUB, :], axis=0, keepdims=True)
@@ -244,33 +260,52 @@
 
     row_i = iota((rows, cols), 0)
     col_i = iota((rows, cols), 1)
-
-    def beside(turn, field):
+    sub16 = iota((4 * tiers, tiers * cols), 0)
+    lane16 = iota((4 * tiers, tiers * cols), 1)
+    put = jnp.where(
+        ((lax.rem(lane16, cols) == 0) & (sub16 == tiers + lane16 // cols))
+        | ((lax.rem(lane16, cols) == cols - 1) & (sub16 == 2 * tiers + lane16 // cols)),
+        1.0,
+        0.0,
+    )
+
+    def inside(field, t):
+        v = field[t]
+        none = jnp.zeros_like(v)
+        low = none if t == 0 else field[t - 1]
+        high = none if t == tiers - 1 else field[t + 1]
+        north = jnp.where(row_i == 0, 0.0, pltpu.roll(v, 1, 0))
+        south = jnp.where(row_i == rows - 1, 0.0, pltpu.roll(v, rows - 1, 0))
+        west = jnp.where(col_i == 0, 0.0, pltpu.roll(v, 1, 1))
+        east = jnp.where(col_i == cols - 1, 0.0, pltpu.roll(v, cols - 1, 1))
+        return v, (low, high, north, south, west, east)
+
+    def rims(turn):
         ends = jnp.concatenate([edge_recv[turn, 2], edge_recv[turn, 3]], axis=0)
-        sub16 = iota((4 * tiers, LANES), 0)
-        lane16 = iota((4 * tiers, LANES), 1)
-        result = []
+        return hi_dot(ends, put, ((0,), (0,)))
+
+    def apply_inside(field, t):
+        v, around = inside(field, t)
+        value = diag[t] * v
+        for k in range(6):
+            if not (k == 0 and t == 0 or k == 1 and t == tiers - 1):
+                value = value - faces[k, t] * around[k]
+        return value
+
+    def add_beyond(turn):
+        rim = rims(turn)
+        resid[0] = resid[0] + faces[0, 0] * plane_recv[turn, 0]
+        resid[tiers - 1] = resid[tiers - 1] + faces[1, tiers - 1] * plane_recv[turn, 1]
         for t in range(tiers):
-            v = field[t]
-            low = plane_recv[turn, 0] if t == 0 else field[t - 1]
-            high = plane_recv[turn, 1] if t == tiers - 1 else field[t + 1]
-            north = jnp.where(
-                row_i == 0, edge_recv[turn, 0, tiers + t : tiers + t + 1, :], pltpu.roll(v, 1, 0)
+            first, last = slice(0, 1), slice(rows - 1, rows)
+            resid[t, first, :] = (
+                resid[t, first, :] + faces[2, t, first, :] * edge_recv[turn, 0, tiers + t : tiers + t + 1, :]
             )
-            south = jnp.where(
-                row_i == rows - 1, edge_recv[turn, 1, t : t + 1, :], pltpu.roll(v, rows - 1, 0)
+            resid[t, last, :] = (
+                resid[t, last, :] + faces[3, t, last, :] * edge_recv[turn, 1, t : t + 1, :]
             )
-            put = jnp.where(
-                ((sub16 == tiers + t) & (lane16 == 0))
-                | ((sub16 == 2 * tiers + t) & (lane16 == cols - 1)),
-                1.0,
-                0.0,
-            )
-            rim = hi_dot(ends, put, ((0,), (0,)))
-            west = jnp.where(col_i == 0, rim, pltpu.roll(v, 1, 1))
-            east = jnp.where(col_i == cols - 1, rim, pltpu.roll(v, cols - 1, 1))
-            result.append((v, (low, high, north, south, west, east)))
-        return result
+            face = jnp.where(col_i == 0, faces[4, t], faces[5, t])
+            resid[t] = resid[t] + face * rim[:, t * cols : (t + 1) * cols]
 
     beyond = (my_layer > 0).astype(jnp.int32) + (my_layer < n_layer - 1).astype(jnp.int32)
     pl.semaphore_wait(barrier, tiles - 1 + beyond)
@@ -305,13 +340,13 @@
     own_copy = pltpu.make_async_copy(note_send.at[own_note, :], note_recv.at[own_note, :], note_rsem.at[0])
     own_copy.start()
 
-    loads[1].wait()
+    loads[6].wait()
     pack_edges(0, temp)
     start_halo(0, temp)
     pack_edges(1, cond)
     start_halo(1, cond)
-    loads[2].wait()
-    loads[3].wait()
+    loads[7].wait()
+    loads[8].wait()
     own_copy.wait()
 
     @pl.loop(1, tiles)
@@ -349,26 +384,29 @@
     own_move = pltpu.make_async_copy(load_send.at[own_load, :], load_recv.at[own_load, :], load_rsem.at[0])
     own_move.start()
 
-    loads[4].wait()
+    loads[9].wait()
     wait_halo(0, temp)
     wait_halo(1, cond)
-    near = beside(1, cond)
+    rim = rims(1)
     for t in range(tiers):
-        c, around = near[t]
+        c, (low, high, north, south, west, east) = inside(cond, t)
+        here = rim[:, t * cols : (t + 1) * cols]
+        low = plane_recv[1, 0] if t == 0 else low
+        high = plane_recv[1, 1] if t == tiers - 1 else high
+        north = jnp.where(row_i == 0, edge_recv[1, 0, tiers + t : tiers + t + 1, :], north)
+        south = jnp.where(row_i == rows - 1, edge_recv[1, 1, t : t + 1, :], south)
+        west = jnp.where(col_i == 0, here, west)
+        east = jnp.where(col_i == cols - 1, here, east)
         total = mass[t]
-        for k in range(6):
-            face = 0.5 * (c + around[k])
+        for k, beside in enumerate((low, high, north, south, west, east)):
+            face = 0.5 * (c + beside)
             faces[k, t] = face
             total = total + face
         diag[t] = total
         inv[t] = 1.0 / total
-    near = beside(0, temp)
     for t in range(tiers):
-        v, around = near[t]
-        value = diag[t] * v
-        for k in range(6):
-            value = value - faces[k, t] * around[k]
-        resid[t] = mass[t] * v - value
+        resid[t] = mass[t] * temp[t] - apply_inside(temp, t)
+    add_beyond(0)
 
     middle = (EIG_LOW + EIG_HIGH) / 2.0
     spread = (EIG_HIGH - EIG_LOW) / 2.0
@@ -410,6 +448,8 @@
             power_ref[pl.ds(at, bands, stride=SUB), :] = jnp.where(left, a, pltpu.roll(b, SUB, 1))
             power_ref[pl.ds(at + 1, bands, stride=SUB), :] = jnp.where(left, pltpu.roll(a, SUB, 1), b)
 
+    power_out = pltpu.make_async_copy(power_ref, power_hbm, out_sem.at[1])
+    power_out.start()
     for t in range(tiers):
         r = resid[t] + power_ref[t * rows : (t + 1) * rows, :]
         resid[t] = r
@@ -419,26 +459,22 @@
         turn = 1 + sweep
         pack_edges(turn, field)
         start_halo(turn, field)
+        weight_new = 1.0 / (2.0 * ratio - weight)
         for t in range(tiers):
             base = temp[t] if sweep == 1 else out_ref[t]
             out_ref[t] = base + field[t]
+            resid[t] = resid[t] - apply_inside(field, t)
         wait_halo(turn, field)
-        weight_new = 1.0 / (2.0 * ratio - weight)
-        near = beside(turn, field)
+        add_beyond(turn)
         for t in range(tiers):
-            v, around = near[t]
-            value = diag[t] * v
-            for k in range(6):
-                value = value - faces[k, t] * around[k]
-            r = resid[t] - value
-            if sweep < SWEEPS - 1:
-                resid[t] = r
-            d = weight_new * weight * v + (2.0 * weight_new / spread) * (r * inv[t])
+            d = weight_new * weight * field[t] + (2.0 * weight_new / spread) * (resid[t] * inv[t])
             if sweep < SWEEPS - 1:
                 dirs[sweep, t] = d
             else:
                 out_ref[t] = out_ref[t] + d
         weight = weight_new
+    out_copy = pltpu.make_async_copy(out_ref, out_hbm, out_sem.at[0])
+    out_copy.start()
 
     end_halo(0, temp)
     end_halo(1, cond)
@@ -449,6 +485,9 @@
     def _(step):
         note_copy(step).wait_send()
         load_copy(step).wait_send()
+
+    power_out.wait()
+    out_copy.wait()
 
 
 def shards(sizes, temp, cond, mass, dyn, leak, panel, place, block, tier, sens):
@@ -458,7 +497,6 @@
     folds = PACK // CAP
     note_rows = -(-(1 + tiles * PACK // LANES) // 8) * 8
     any_spec = pl.BlockSpec(memory_space=pl.ANY)
-    vmem = pl.BlockSpec(memory_space=pltpu.VMEM)
     grid = (tiers, rows, cols)
     dma = pltpu.SemaphoreType.DMA
     new, power = pl.pallas_call(
@@ -467,9 +505,16 @@
             jax.ShapeDtypeStruct(grid, F32),
             jax.ShapeDtypeStruct((tiers * rows, cols), F32),
         ),
-        in_specs=[any_spec] * 5 + [vmem] * 5,
-        out_specs=(vmem, vmem),
+        in_specs=[any_spec] * 10,
+        out_specs=(any_spec, any_spec),
         scratch_shapes=[
+            pltpu.VMEM((1, slots), jnp.int32),
+            pltpu.VMEM((1, slots), jnp.int32),
+            pltpu.VMEM((1, slots), jnp.int32),
+            pltpu.VMEM(tier.shape, jnp.int32),
+            pltpu.VMEM(sens.shape, F32),
+            pltpu.VMEM(grid, F32),
+            pltpu.VMEM((tiers * rows, cols), F32),
             pltpu.VMEM(grid, F32),
             pltpu.VMEM(grid, F32),
             pltpu.VMEM(grid, F32),
@@ -487,7 +532,8 @@
             pltpu.VMEM((SWEEPS + 1, 2, 2 * tiers, cols), F32),
             pltpu.VMEM((SWEEPS + 1, 4, 2 * tiers, cols), F32),
             pltpu.VMEM((SWEEPS + 1, 2, rows, cols), F32),
-            dma((5,)),
+            dma((10,)),
+            dma((2,)),
             dma((tiles,)),
             dma((tiles,)),
             dma((tiles,)),
@@ -496,9 +542,9 @@
             dma((SWEEPS + 1, 6)),
         ],
         compiler_params=pltpu.CompilerParams(
-            collective_id=0, has_side_effects=True, vmem_limit_bytes=48 * 1024 * 1024
+            collective_id=0, has_side_effects=True, vmem_limit_bytes=VMEM_BYTES
         ),
-    )(temp, cond, mass, dyn, leak, panel[0], place, block, tier, sens)
+    )(temp, cond, mass, dyn, leak, panel.reshape(1, slots), place, block, tier, sens)
     return new, power.reshape(grid)
 
 

time: 43.5 us -> 38.5 us (0.89)
  local copies, waits for them, and re-layouts: 7.68 us -> 2.42 us
    unnamed x22 -> x4, local copies, waits for them, and re-layouts: 7.59 us -> 2.42 us
    pallas_call x1, Pallas kernels: 34.8 us -> 35.2 us  [shards(): pl.pallas_call(functools.partial(kernel, sizes), out_shape=(jax.ShapeDtyp...]
where the time goes in v2:
time: 38.5 us; the launch traced here: 38.3 us
  Pallas kernels  35.2 us (91%)
  local copies, waits for them, and re-layouts  2.42 us (6%)
  between operations  0.65 us (2%)
    pallas_call x1, Pallas kernels, shards(): pl.pallas_call(functools.partial(kernel, sizes), out_shape=(jax.ShapeDtyp...  35.2 us
    unnamed x4, local copies, waits for them, and re-layouts  2.42 us

profile of v2, /device:TPU:0, one launch (start us, length us, event | category | flops | bytes accessed | tf_op | source)
XLA Modules:
  0.0 38.3 jit_solution(17079081988016129832)
XLA Ops:
  0.6 35.2 %shard_map.113 = (f32[4,128,128]{2,1,0:T(8,128)}, f32[512,128]{1,0:T(8,128)}) custom-call(f32[4,128,128]{2,1,0:T(8,128)} %temp_hbm.1, f32[4,128,128]{2,1,0:T(8,128)} %cond_hbm.1, f32[4,128,128]{2,1,0:T(8,128)} %mass_hbm.1, bf16[1,64,4096]{2,1,0:T(8,128)(2,1)} %dyn_hbm.1, bf16[1,64,4096]{2,1,0:T(8,128)(2,1)} %leak_hbm.1, s32[1,64]{1,0:T(1,128)} %bitcast.3, ...), custom_call_target="tpu_custom_call" | custom-call | tf_op jit(solution)/shard_map/pallas_call | solution.py:502
  35.9 0.0 copy-start
  35.9 1.7 %copy.14 = f32[4,128,128]{2,1,0:T(8,128)} copy(f32[4,128,128]{2,1,0:T(8,128)} %get-tuple-element.8) | data formatting | bytes 524288
  37.6 0.0 copy-done
  37.6 0.7 %copy.15 = f32[4,128,128]{2,1,0:T(8,128)} copy(f32[4,128,128]{2,1,0:T(8,128)S(1)} %bitcast.2) | data formatting | bytes 524288
Async XLA Ops:
  35.9 1.7 %copy-start = (f32[512,128]{1,0:T(8,128)S(1)}, f32[512,128]{1,0:T(8,128)}, u32[]{:S(2)}) copy-start(f32[512,128]{1,0:T(8,128)} %get-tuple-element.5) | copy-start | bytes 786436

commit v3 on v2

--- a/solution.py
+++ b/solution.py
@@ -28,6 +28,23 @@
     return lax.dot_general(
         a, b, (dims, ((), ())), precision=lax.Precision.HIGHEST, preferred_element_type=F32
     )
+
+
+def div(x, n):
+    if n & (n - 1):
+        return x // n
+    return lax.shift_right_logical(x, jnp.int32(n.bit_length() - 1))
+
+
+def mod(x, n):
+    if n & (n - 1):
+        return lax.rem(x, n)
+    return x & (n - 1)
+
+
+def two_parts(x, axis):
+    head = x.astype(BF16)
+    return jnp.concatenate([head, (x - head.astype(F32)).astype(BF16)], axis=axis)
 
 
 def kernel(
@@ -185,7 +202,7 @@
     place_lanes = jnp.where(fits, pos_col + 1.0, 0.0)
     note_i = iota((tiles * note_rows, slots), 0)
     to_tile = jnp.where(
-        ((note_i // note_rows).astype(F32) == tgt_row) & (lax.rem(note_i, note_rows) == 1 + my_chunk),
+        (div(note_i, note_rows).astype(F32) == tgt_row) & (mod(note_i, note_rows) == 1 + my_chunk),
         1.0,
         0.0,
     )
@@ -205,16 +222,22 @@
     means = jnp.zeros((1, LANES), F32)
     per_band = cols // SUB
     for part in range(per_band):
-        total = jnp.sum(jnp.where(lane_b // SUB == part, band_sums, 0.0), axis=1, keepdims=True)
+        total = jnp.sum(jnp.where(div(lane_b, SUB) == part, band_sums, 0.0), axis=1, keepdims=True)
         means = means + jnp.sum(
             jnp.where(lane_b == sub_b * per_band + part, total, 0.0), axis=0, keepdims=True
         )
     means = means * (1.0 / (SUB * SUB))
     note_j = iota((tiles * note_rows, LANES), 0)
-    note_send[...] = places + jnp.where(lax.rem(note_j, note_rows) == 0, means, 0.0)
-
-    sub8 = iota((2 * tiers, LANES), 0)
-    lane8 = iota((2 * tiers, LANES), 1)
+    note_send[...] = places + jnp.where(mod(note_j, note_rows) == 0, means, 0.0)
+
+    sub8 = iota((2 * tiers, 2 * cols), 0)
+    lane8 = mod(iota((2 * tiers, 2 * cols), 1), cols)
+    picks = [
+        jnp.where(
+            ((sub8 == t) & (lane8 == 0)) | ((sub8 == tiers + t) & (lane8 == cols - 1)), 1.0, 0.0
+        ).astype(BF16)
+        for t in range(tiers)
+    ]
 
     def halo_copy(turn, field, where, side, lands):
         if side < 2:
@@ -239,10 +262,9 @@
                 edge_send[turn, 0, end * tiers + t : end * tiers + t + 1, :] = field[t, at : at + 1, :]
         columns = jnp.zeros((2 * tiers, rows), F32)
         for t in range(tiers):
-            pick = jnp.where(
-                ((sub8 == t) & (lane8 == 0)) | ((sub8 == tiers + t) & (lane8 == cols - 1)), 1.0, 0.0
+            columns = columns + lax.dot_general(
+                picks[t], two_parts(field[t], 1), (((1,), (1,)), ((), ())), preferred_element_type=F32
             )
-            columns = columns + hi_dot(pick, field[t], ((1,), (1,)))
         edge_send[turn, 1] = columns
 
     def each_side(act):
@@ -260,14 +282,14 @@
 
     row_i = iota((rows, cols), 0)
     col_i = iota((rows, cols), 1)
-    sub16 = iota((4 * tiers, tiers * cols), 0)
-    lane16 = iota((4 * tiers, tiers * cols), 1)
+    sub16 = mod(iota((8 * tiers, tiers * cols), 0), 4 * tiers)
+    lane16 = iota((8 * tiers, tiers * cols), 1)
     put = jnp.where(
-        ((lax.rem(lane16, cols) == 0) & (sub16 == tiers + lane16 // cols))
-        | ((lax.rem(lane16, cols) == cols - 1) & (sub16 == 2 * tiers + lane16 // cols)),
+        ((mod(lane16, cols) == 0) & (sub16 == tiers + div(lane16, cols)))
+        | ((mod(lane16, cols) == cols - 1) & (sub16 == 2 * tiers + div(lane16, cols))),
         1.0,
         0.0,
-    )
+    ).astype(BF16)
 
     def inside(field, t):
         v = field[t]
@@ -282,7 +304,9 @@
 
     def rims(turn):
         ends = jnp.concatenate([edge_recv[turn, 2], edge_recv[turn, 3]], axis=0)
-        return hi_dot(ends, put, ((0,), (0,)))
+        return lax.dot_general(
+            two_parts(ends, 0), put, (((0,), (0,)), ((), ())), preferred_element_type=F32
+        )
 
     def apply_inside(field, t):
         v, around = inside(field, t)
@@ -347,34 +371,42 @@
     start_halo(1, cond)
     loads[7].wait()
     loads[8].wait()
+    note_k = iota((slots, tiles * note_rows), 1)
+    from_tile = jnp.where(
+        (div(note_k, note_rows).astype(F32) == tgt_col) & (mod(note_k, note_rows) == 0), 1.0, 0.0
+    )
+    at_place = iota((slots, LANES), 1).astype(F32) == pos_col
+    send_i = iota((tiles * PACK, folds * slots), 0)
+    send_j = iota((tiles * PACK, folds * slots), 1)
+    slot_place = jnp.concatenate([tgt_row * CAP + rank_row] * folds, axis=1)
+    goes = (div(send_i, PACK) * CAP + mod(send_i, CAP)).astype(F32) == slot_place
+    pick = jnp.where(goes & (div(mod(send_i, PACK), CAP) == div(send_j, slots)), 1.0, 0.0).astype(BF16)
     own_copy.wait()
 
     @pl.loop(1, tiles)
     def _(step):
         note_copy(step).wait_recv()
 
-    note_k = iota((slots, tiles * note_rows), 1)
-    from_tile = jnp.where(
-        ((note_k // note_rows).astype(F32) == tgt_col) & (lax.rem(note_k, note_rows) == 0), 1.0, 0.0
-    )
     tile_means = hi_dot(from_tile, note_recv[...], ((1,), (0,)))
-    slot_mean = jnp.sum(
-        jnp.where(iota((slots, LANES), 1).astype(F32) == pos_col, tile_means, 0.0), axis=1, keepdims=True
-    )
+    slot_mean = jnp.sum(jnp.where(at_place, tile_means, 0.0), axis=1, keepdims=True)
     block_rise = jnp.sum(same_block * to_row(slot_mean), axis=1, keepdims=True) / block_size
     factor = jnp.exp(sens_col * block_rise)
-    send_i = iota((tiles * PACK, slots), 0)
-    goes = (
-        (send_i // PACK) * CAP + lax.rem(send_i, CAP)
-    ).astype(F32) == tgt_row * CAP + rank_row
-    fold_i = lax.rem(send_i, PACK) // CAP
-    gathered = jnp.zeros((tiles * PACK, wide), F32)
-    for fold in range(folds):
-        part = slice(fold * wide, (fold + 1) * wide)
-        slot_power = (dyn[:, part].astype(F32) + factor * leak[:, part].astype(F32)).astype(BF16)
-        pick = jnp.where(goes & (fold_i == fold), 1.0, 0.0).astype(BF16)
-        gathered = gathered + jnp.dot(pick, slot_power, preferred_element_type=F32)
-    load_send[...] = gathered.astype(BF16)
+    half = wide // 2
+    for piece in range(2):
+        slot_power = jnp.concatenate(
+            [
+                (
+                    dyn[:, fold * wide + piece * half : fold * wide + (piece + 1) * half].astype(F32)
+                    + factor
+                    * leak[:, fold * wide + piece * half : fold * wide + (piece + 1) * half].astype(F32)
+                ).astype(BF16)
+                for fold in range(folds)
+            ],
+            axis=0,
+        )
+        load_send[:, piece * half : (piece + 1) * half] = jnp.dot(
+            pick, slot_power, preferred_element_type=F32
+        ).astype(BF16)
 
     @pl.loop(1, tiles)
     def _(step):
@@ -415,29 +447,25 @@
 
     sel_i = iota((folds * patches, LANES), 0)
     sel_j = iota((folds * patches, LANES), 1)
-    sel_fold = sel_i // patches
-    sel_in = lax.rem(sel_i, patches)
-    sel_patch = lax.rem(sel_in, bands) * per_band + sel_in // bands
-    fold_hit = sel_fold == lax.rem(sel_j, PACK) // CAP
+    sel_in = mod(sel_i, patches)
+    sel_patch = mod(sel_in, bands) * per_band + div(sel_in, bands)
+    fold_hit = div(sel_i, patches) == div(mod(sel_j, PACK), CAP)
     notes = note_recv[...]
     pickers = []
     for chunk in range(chunks):
-        code = jnp.sum(jnp.where(lax.rem(note_j, note_rows) == 1 + chunk, notes, 0.0), axis=0, keepdims=True)
+        code = jnp.sum(jnp.where(mod(note_j, note_rows) == 1 + chunk, notes, 0.0), axis=0, keepdims=True)
         pickers.append(
             jnp.where(fold_hit & (code == (sel_patch + 1).astype(F32)), 1.0, 0.0).astype(BF16)
         )
 
+    picker = jnp.concatenate(pickers, axis=1)
     own_move.wait()
 
     @pl.loop(1, tiles)
     def _(step):
         load_copy(step).wait_recv()
 
-    footprint = jnp.zeros((folds * patches, wide), F32)
-    for chunk in range(chunks):
-        footprint = footprint + jnp.dot(
-            pickers[chunk], load_recv[chunk * LANES : (chunk + 1) * LANES, :], preferred_element_type=F32
-        )
+    footprint = jnp.dot(picker, load_recv[...], preferred_element_type=F32)
     left = iota((bands, LANES), 1) < SUB
     for fold in range(folds):
         for k in range(wide // LANES):

time: 38.5 us -> 35.9 us (0.932)
  Pallas kernels: 35.2 us -> 32.7 us
    pallas_call x1, Pallas kernels: 35.2 us -> 32.7 us  [shards(): pl.pallas_call(functools.partial(kernel, sizes), out_shape=(jax.ShapeDtyp...]
where the time goes in v3:
time: 35.9 us; the launch traced here: 35.8 us
  Pallas kernels  32.7 us (91%)
  local copies, waits for them, and re-layouts  2.42 us (7%)
  between operations  0.65 us (2%)
    pallas_call x1, Pallas kernels, shards(): pl.pallas_call(functools.partial(kernel, sizes), out_shape=(jax.ShapeDtyp...  32.7 us
    unnamed x4, local copies, waits for them, and re-layouts  2.42 us

profile of v3, /device:TPU:0, one launch (start us, length us, event | category | flops | bytes accessed | tf_op | source)
XLA Modules:
  0.0 35.8 jit_solution(17726045701535381983)
XLA Ops:
  0.6 32.7 %shard_map.113 = (f32[4,128,128]{2,1,0:T(8,128)}, f32[512,128]{1,0:T(8,128)}) custom-call(f32[4,128,128]{2,1,0:T(8,128)} %temp_hbm.1, f32[4,128,128]{2,1,0:T(8,128)} %cond_hbm.1, f32[4,128,128]{2,1,0:T(8,128)} %mass_hbm.1, bf16[1,64,4096]{2,1,0:T(8,128)(2,1)} %dyn_hbm.1, bf16[1,64,4096]{2,1,0:T(8,128)(2,1)} %leak_hbm.1, s32[1,64]{1,0:T(1,128)} %bitcast.3, ...), custom_call_target="tpu_custom_call" | custom-call | tf_op jit(solution)/shard_map/pallas_call | solution.py:530
  33.4 0.0 copy-start
  33.4 1.7 %copy.14 = f32[4,128,128]{2,1,0:T(8,128)} copy(f32[4,128,128]{2,1,0:T(8,128)} %get-tuple-element.8) | data formatting | bytes 524288
  35.1 0.0 copy-done
  35.1 0.7 %copy.15 = f32[4,128,128]{2,1,0:T(8,128)} copy(f32[4,128,128]{2,1,0:T(8,128)S(1)} %bitcast.2) | data formatting | bytes 524288
Async XLA Ops:
  33.4 1.7 %copy-start = (f32[512,128]{1,0:T(8,128)S(1)}, f32[512,128]{1,0:T(8,128)}, u32[]{:S(2)}) copy-start(f32[512,128]{1,0:T(8,128)} %get-tuple-element.5) | copy-start | bytes 786436

commit v4 on v3

--- a/solution.py
+++ b/solution.py
@@ -255,11 +255,13 @@
             device_id_type=MESH,
         )
 
-    def pack_edges(turn, field):
+    def pack_rows(turn, field):
         for end in range(2):
             at = end * (rows - 1)
             for t in range(tiers):
                 edge_send[turn, 0, end * tiers + t : end * tiers + t + 1, :] = field[t, at : at + 1, :]
+
+    def pack_columns(turn, field):
         columns = jnp.zeros((2 * tiers, rows), F32)
         for t in range(tiers):
             columns = columns + lax.dot_general(
@@ -267,12 +269,19 @@
             )
         edge_send[turn, 1] = columns
 
-    def each_side(act):
-        for exists, where, side in sides:
+    def each_side(act, which=sides):
+        for exists, where, side in which:
             pl.when(exists)(functools.partial(act, where, side))
 
     def start_halo(turn, field):
-        each_side(lambda where, side: halo_copy(turn, field, where, side, side ^ 1).start())
+        def start(where, side):
+            halo_copy(turn, field, where, side, side ^ 1).start()
+
+        pack_rows(turn, field)
+        each_side(start, sides[2:4])
+        each_side(start, sides[:2])
+        pack_columns(turn, field)
+        each_side(start, sides[4:])
 
     def wait_halo(turn, field):
         each_side(lambda where, side: halo_copy(turn, field, where, side, side).wait_recv())
@@ -345,14 +354,13 @@
             device_id_type=MESH,
         )
 
-    def load_copy(step):
-        other, where = peer(step)
+    def load_copy(other, lands):
         return pltpu.make_async_remote_copy(
             src_ref=load_send.at[pl.ds(other * PACK, PACK), :],
             dst_ref=load_recv.at[pl.ds(me * PACK, PACK), :],
-            send_sem=load_ssem.at[step],
-            recv_sem=load_rsem.at[step],
-            device_id=where,
+            send_sem=load_ssem.at[other],
+            recv_sem=load_rsem.at[lands],
+            device_id={"row": div(other, n_col), "col": mod(other, n_col)},
             device_id_type=MESH,
         )
 
@@ -365,9 +373,7 @@
     own_copy.start()
 
     loads[6].wait()
-    pack_edges(0, temp)
     start_halo(0, temp)
-    pack_edges(1, cond)
     start_halo(1, cond)
     loads[7].wait()
     loads[8].wait()
@@ -408,12 +414,18 @@
             pick, slot_power, preferred_element_type=F32
         ).astype(BF16)
 
-    @pl.loop(1, tiles)
+    @pl.loop(0, tiles)
     def _(step):
-        load_copy(step).start()
+        nth = div(step, n_row)
+        far = jnp.where(my_col < n_col // 2, n_col - 1 - nth, nth)
+        other = lax.rem(my_row + lax.rem(step, n_row), n_row) * n_col + far
+
+        @pl.when(other != me)
+        def _():
+            load_copy(other, me).start()
 
     own_load = pl.ds(pl.multiple_of(me * PACK, PACK), PACK)
-    own_move = pltpu.make_async_copy(load_send.at[own_load, :], load_recv.at[own_load, :], load_rsem.at[0])
+    own_move = pltpu.make_async_copy(load_send.at[own_load, :], load_recv.at[own_load, :], load_rsem.at[me])
     own_move.start()
 
     loads[9].wait()
@@ -463,7 +475,8 @@
 
     @pl.loop(1, tiles)
     def _(step):
-        load_copy(step).wait_recv()
+        other, _ = peer(step)
+        load_copy(other, other).wait_recv()
 
     footprint = jnp.dot(picker, load_recv[...], preferred_element_type=F32)
     left = iota((bands, LANES), 1) < SUB
@@ -485,7 +498,6 @@
     for sweep in range(1, SWEEPS):
         field = dirs.at[sweep - 1]
         turn = 1 + sweep
-        pack_edges(turn, field)
         start_halo(turn, field)
         weight_new = 1.0 / (2.0 * ratio - weight)
         for t in range(tiers):
@@ -512,10 +524,24 @@
     @pl.loop(1, tiles)
     def _(step):
         note_copy(step).wait_send()
-        load_copy(step).wait_send()
+        other, _ = peer(step)
+        load_copy(other, me).wait_send()
 
     power_out.wait()
     out_copy.wait()
+
+
+def hand_over(new, power, new_out, power_out, held, sem):
+    pairs = ((power, power_out), (new, new_out))
+    takes = [pltpu.make_async_copy(src, held.at[i], sem.at[0, i]) for i, (src, _) in enumerate(pairs)]
+    gives = [pltpu.make_async_copy(held.at[i], dst, sem.at[1, i]) for i, (_, dst) in enumerate(pairs)]
+    for take in takes:
+        take.start()
+    for take, give in zip(takes, gives):
+        take.wait()
+        give.start()
+    for give in gives:
+        give.wait()
 
 
 def shards(sizes, temp, cond, mass, dyn, leak, panel, place, block, tier, sens):
@@ -573,7 +599,14 @@
             collective_id=0, has_side_effects=True, vmem_limit_bytes=VMEM_BYTES
         ),
     )(temp, cond, mass, dyn, leak, panel.reshape(1, slots), place, block, tier, sens)
-    return new, power.reshape(grid)
+    return pl.pallas_call(
+        hand_over,
+        out_shape=(jax.ShapeDtypeStruct(grid, F32),) * 2,
+        in_specs=[any_spec] * 2,
+        out_specs=(any_spec, any_spec),
+        scratch_shapes=[pltpu.VMEM((2,) + grid, F32), dma((2, 2))],
+        compiler_params=pltpu.CompilerParams(vmem_limit_bytes=VMEM_BYTES),
+    )(new, power.reshape(grid))
 
 
 def solution(mesh):

time: 35.9 us -> 35.3 us (0.983)
  local copies, waits for them, and re-layouts: 2.42 us -> 0 us
  Pallas kernels: 32.7 us -> 34.5 us
    unnamed x4 -> x0, local copies, waits for them, and re-layouts: 2.42 us -> none
    pallas_call x0 -> x1, Pallas kernels: none -> 1.77 us  [shards(): pl.pallas_call(hand_over, out_shape=(jax.ShapeDtypeStruct(grid, F32),) *...]
where the time goes in v4:
time: 35.3 us; the launch traced here: 35.2 us
  Pallas kernels  34.5 us (98%)
  between operations  0.64 us (2%)
    pallas_call x1, Pallas kernels, shards(): pl.pallas_call(functools.partial(kernel, sizes), out_shape=(jax.ShapeDtyp...  32.8 us
    pallas_call x1, Pallas kernels, shards(): pl.pallas_call(hand_over, out_shape=(jax.ShapeDtypeStruct(grid, F32),) *...  1.77 us

profile of v4, /device:TPU:0, one launch (start us, length us, event | category | flops | bytes accessed | tf_op | source)
XLA Modules:
  0.0 35.2 jit_solution(14706787896092029753)
XLA Ops:
  0.6 32.8 %shard_map.113 = (f32[4,128,128]{2,1,0:T(8,128)}, f32[512,128]{1,0:T(8,128)}) custom-call(f32[4,128,128]{2,1,0:T(8,128)} %temp_hbm.1, f32[4,128,128]{2,1,0:T(8,128)} %cond_hbm.1, f32[4,128,128]{2,1,0:T(8,128)} %mass_hbm.1, bf16[1,64,4096]{2,1,0:T(8,128)(2,1)} %dyn_hbm.1, bf16[1,64,4096]{2,1,0:T(8,128)(2,1)} %leak_hbm.1, s32[1,64]{1,0:T(1,128)} %bitcast.3, ...), custom_call_target="tpu_custom_call" | custom-call | tf_op jit(solution)/shard_map/pallas_call | solution.py:556
  33.4 1.8 %shard_map.114 = (f32[4,128,128]{2,1,0:T(8,128)}, f32[4,128,128]{2,1,0:T(8,128)}) custom-call(f32[4,128,128]{2,1,0:T(8,128)} %get-tuple-element.4.new, f32[4,128,128]{2,1,0:T(8,128)} %bitcast.2), custom_call_target="tpu_custom_call" | custom-call | tf_op jit(solution)/shard_map/pallas_call | solution.py:602

commit v5 on v4

--- a/solution.py
+++ b/solution.py
@@ -354,14 +354,25 @@
             device_id_type=MESH,
         )
 
-    def load_copy(other, lands):
+    half = wide // 2
+
+    def load_copy(piece, other, lands):
+        part = slice(piece * half, (piece + 1) * half)
         return pltpu.make_async_remote_copy(
-            src_ref=load_send.at[pl.ds(other * PACK, PACK), :],
-            dst_ref=load_recv.at[pl.ds(me * PACK, PACK), :],
-            send_sem=load_ssem.at[other],
-            recv_sem=load_rsem.at[lands],
+            src_ref=load_send.at[pl.ds(other * PACK, PACK), part],
+            dst_ref=load_recv.at[pl.ds(me * PACK, PACK), part],
+            send_sem=load_ssem.at[piece, other],
+            recv_sem=load_rsem.at[piece, lands],
             device_id={"row": div(other, n_col), "col": mod(other, n_col)},
             device_id_type=MESH,
+        )
+
+    own_load = pl.ds(pl.multiple_of(me * PACK, PACK), PACK)
+
+    def own_move(piece):
+        part = slice(piece * half, (piece + 1) * half)
+        return pltpu.make_async_copy(
+            load_send.at[own_load, part], load_recv.at[own_load, part], load_rsem.at[piece, me]
         )
 
     @pl.loop(1, tiles)
@@ -381,6 +392,7 @@
     from_tile = jnp.where(
         (div(note_k, note_rows).astype(F32) == tgt_col) & (mod(note_k, note_rows) == 0), 1.0, 0.0
     )
+    from_tile = jnp.concatenate([from_tile.astype(BF16)] * 3, axis=1)
     at_place = iota((slots, LANES), 1).astype(F32) == pos_col
     send_i = iota((tiles * PACK, folds * slots), 0)
     send_j = iota((tiles * PACK, folds * slots), 1)
@@ -393,11 +405,14 @@
     def _(step):
         note_copy(step).wait_recv()
 
-    tile_means = hi_dot(from_tile, note_recv[...], ((1,), (0,)))
+    head = note_recv[...].astype(BF16)
+    rest = note_recv[...] - head.astype(F32)
+    tile_means = jnp.dot(
+        from_tile, jnp.concatenate([head, two_parts(rest, 0)], axis=0), preferred_element_type=F32
+    )
     slot_mean = jnp.sum(jnp.where(at_place, tile_means, 0.0), axis=1, keepdims=True)
     block_rise = jnp.sum(same_block * to_row(slot_mean), axis=1, keepdims=True) / block_size
     factor = jnp.exp(sens_col * block_rise)
-    half = wide // 2
     for piece in range(2):
         slot_power = jnp.concatenate(
             [
@@ -414,19 +429,17 @@
             pick, slot_power, preferred_element_type=F32
         ).astype(BF16)
 
-    @pl.loop(0, tiles)
-    def _(step):
-        nth = div(step, n_row)
-        far = jnp.where(my_col < n_col // 2, n_col - 1 - nth, nth)
-        other = lax.rem(my_row + lax.rem(step, n_row), n_row) * n_col + far
-
-        @pl.when(other != me)
-        def _():
-            load_copy(other, me).start()
-
-    own_load = pl.ds(pl.multiple_of(me * PACK, PACK), PACK)
-    own_move = pltpu.make_async_copy(load_send.at[own_load, :], load_recv.at[own_load, :], load_rsem.at[me])
-    own_move.start()
+        @pl.loop(0, tiles)
+        def _(step, piece=piece):
+            nth = div(step, n_row)
+            far = jnp.where(my_col < n_col // 2, n_col - 1 - nth, nth)
+            other = lax.rem(my_row + lax.rem(step, n_row), n_row) * n_col + far
+
+            @pl.when(other != me)
+            def _():
+                load_copy(piece, other, me).start()
+
+        own_move(piece).start()
 
     loads[9].wait()
     wait_halo(0, temp)
@@ -471,25 +484,33 @@
         )
 
     picker = jnp.concatenate(pickers, axis=1)
-    own_move.wait()
-
-    @pl.loop(1, tiles)
-    def _(step):
-        other, _ = peer(step)
-        load_copy(other, other).wait_recv()
-
-    footprint = jnp.dot(picker, load_recv[...], preferred_element_type=F32)
     left = iota((bands, LANES), 1) < SUB
-    for fold in range(folds):
-        for k in range(wide // LANES):
-            lanes = slice(k * LANES, (k + 1) * LANES)
-            a = footprint[fold * patches : fold * patches + bands, lanes]
-            b = footprint[fold * patches + bands : fold * patches + 2 * bands, lanes]
-            at = 2 * (fold * (wide // LANES) + k)
-            power_ref[pl.ds(at, bands, stride=SUB), :] = jnp.where(left, a, pltpu.roll(b, SUB, 1))
-            power_ref[pl.ds(at + 1, bands, stride=SUB), :] = jnp.where(left, pltpu.roll(a, SUB, 1), b)
-
-    power_out = pltpu.make_async_copy(power_ref, power_hbm, out_sem.at[1])
+    for piece in range(2):
+        own_move(piece).wait()
+
+        @pl.loop(1, tiles)
+        def _(step, piece=piece):
+            other, _ = peer(step)
+            load_copy(piece, other, other).wait_recv()
+
+        footprint = jnp.dot(
+            picker, load_recv[:, piece * half : (piece + 1) * half], preferred_element_type=F32
+        )
+        for fold in range(folds):
+            for k in range(half // LANES):
+                lanes = slice(k * LANES, (k + 1) * LANES)
+                a = footprint[fold * patches : fold * patches + bands, lanes]
+                b = footprint[fold * patches + bands : fold * patches + 2 * bands, lanes]
+                at = 2 * (fold * (wide // LANES) + piece * (half // LANES) + k)
+                power_ref[pl.ds(at, bands, stride=SUB), :] = jnp.where(left, a, pltpu.roll(b, SUB, 1))
+                power_ref[pl.ds(at + 1, bands, stride=SUB), :] = jnp.where(
+                    left, pltpu.roll(a, SUB, 1), b
+                )
+
+    def out_copy(t):
+        return pltpu.make_async_copy(out_ref.at[t], out_hbm.at[t], out_sem.at[t])
+
+    power_out = pltpu.make_async_copy(power_ref, power_hbm, out_sem.at[tiers])
     power_out.start()
     for t in range(tiers):
         r = resid[t] + power_ref[t * rows : (t + 1) * rows, :]
@@ -512,10 +533,8 @@
                 dirs[sweep, t] = d
             else:
                 out_ref[t] = out_ref[t] + d
+                out_copy(t).start()
         weight = weight_new
-    out_copy = pltpu.make_async_copy(out_ref, out_hbm, out_sem.at[0])
-    out_copy.start()
-
     end_halo(0, temp)
     end_halo(1, cond)
     for sweep in range(1, SWEEPS):
@@ -525,16 +544,19 @@
     def _(step):
         note_copy(step).wait_send()
         other, _ = peer(step)
-        load_copy(other, me).wait_send()
+        load_copy(0, other, me).wait_send()
+        load_copy(1, other, me).wait_send()
 
     power_out.wait()
-    out_copy.wait()
+    for t in range(tiers):
+        out_copy(t).wait()
 
 
 def hand_over(new, power, new_out, power_out, held, sem):
-    pairs = ((power, power_out), (new, new_out))
-    takes = [pltpu.make_async_copy(src, held.at[i], sem.at[0, i]) for i, (src, _) in enumerate(pairs)]
-    gives = [pltpu.make_async_copy(held.at[i], dst, sem.at[1, i]) for i, (_, dst) in enumerate(pairs)]
+    planes = [(i, t) for i in range(2) for t in range(new.shape[0])]
+    src, dst = (power, new), (power_out, new_out)
+    takes = [pltpu.make_async_copy(src[i].at[t], held.at[i, t], sem.at[0, i, t]) for i, t in planes]
+    gives = [pltpu.make_async_copy(held.at[i, t], dst[i].at[t], sem.at[1, i, t]) for i, t in planes]
     for take in takes:
         take.start()
     for take, give in zip(takes, gives):
@@ -587,11 +609,11 @@
             pltpu.VMEM((SWEEPS + 1, 4, 2 * tiers, cols), F32),
             pltpu.VMEM((SWEEPS + 1, 2, rows, cols), F32),
             dma((10,)),
-            dma((2,)),
+            dma((tiers + 1,)),
             dma((tiles,)),
             dma((tiles,)),
-            dma((tiles,)),
-            dma((tiles,)),
+            dma((2, tiles)),
+            dma((2, tiles)),
             dma((SWEEPS + 1, 6)),
             dma((SWEEPS + 1, 6)),
         ],
@@ -604,7 +626,7 @@
         out_shape=(jax.ShapeDtypeStruct(grid, F32),) * 2,
         in_specs=[any_spec] * 2,
         out_specs=(any_spec, any_spec),
-        scratch_shapes=[pltpu.VMEM((2,) + grid, F32), dma((2, 2))],
+        scratch_shapes=[pltpu.VMEM((2,) + grid, F32), dma((2, 2, tiers))],
         compiler_params=pltpu.CompilerParams(vmem_limit_bytes=VMEM_BYTES),
     )(new, power.reshape(grid))
 

time: 35.3 us -> 35.4 us (level)
  no operation moved by 1% of the time
where the time goes in v5:
time: 35.4 us; the launch traced here: 35.2 us
  Pallas kernels  34.6 us (98%)
  between operations  0.64 us (2%)
    pallas_call x1, Pallas kernels, shards(): pl.pallas_call(functools.partial(kernel, sizes), out_shape=(jax.ShapeDtyp...  32.7 us
    pallas_call x1, Pallas kernels, shards(): pl.pallas_call(hand_over, out_shape=(jax.ShapeDtypeStruct(grid, F32),) *...  1.83 us

profile of v5, /device:TPU:0, one launch (start us, length us, event | category | flops | bytes accessed | tf_op | source)
XLA Modules:
  0.0 35.2 jit_solution(358180294359327553)
XLA Ops:
  0.6 32.7 %shard_map.113 = (f32[4,128,128]{2,1,0:T(8,128)}, f32[512,128]{1,0:T(8,128)}) custom-call(f32[4,128,128]{2,1,0:T(8,128)} %temp_hbm.1, f32[4,128,128]{2,1,0:T(8,128)} %cond_hbm.1, f32[4,128,128]{2,1,0:T(8,128)} %mass_hbm.1, bf16[1,64,4096]{2,1,0:T(8,128)(2,1)} %dyn_hbm.1, bf16[1,64,4096]{2,1,0:T(8,128)(2,1)} %leak_hbm.1, s32[1,64]{1,0:T(1,128)} %bitcast.3, ...), custom_call_target="tpu_custom_call" | custom-call | tf_op jit(solution)/shard_map/pallas_call | solution.py:578
  33.4 1.8 %shard_map.114 = (f32[4,128,128]{2,1,0:T(8,128)}, f32[4,128,128]{2,1,0:T(8,128)}) custom-call(f32[4,128,128]{2,1,0:T(8,128)} %get-tuple-element.4.new, f32[4,128,128]{2,1,0:T(8,128)} %bitcast.2), custom_call_target="tpu_custom_call" | custom-call | tf_op jit(solution)/shard_map/pallas_call | solution.py:624
